TPU v7x, 32 devices: a whole 2x2x4 slice. The times are simulated.
32 devices in a mesh: row: 4 (over y, x), col: 4 (over z), layer: 2 (over core).
Axes of the slice: x: 2, y: 2, z: 4, core: 2. Of those that a mesh axis runs over, the one named last changes fastest.
Arguments:
- blocks: float32 [4, 4, 2, 8, 128, 128], P('row', 'col', 'layer'), may hold values from -0.5 to 0.5
- block_ids: int32 [4, 4, 2, 8], P('row', 'col', 'layer'), may hold values from 0 to 143, as said below
- counts: int32 [4, 4, 2], P('row', 'col', 'layer'), may hold values from 0 to 8, as said below
Outputs:
- purified: float32 [6144, 6144], P(('row', 'layer'), 'col')
Inputs may be any that keep to these rules, and one draw needn't show every extreme that they name: `block_ids`: within one tile the 2 x 8 slots named over all layers are distinct. `counts`: A tile's live blocks fill the list of layer 0 before that of the next layer; some device's list is full in every draw.
All inputs are finite; a program needn't handle non-finite values.
Results may differ from a plain program's by a relative error of at most 0.000075.
Values sent between devices are 32-bit elements; how exact they have to be, the bound alone decides.
No kernel may reach another device: no remote copies, remote signals or barrier semaphores. Data moves between devices by JAX's collectives and lax.ppermute only.
A program may use at most 320 MiB of HBM per device.

v0:
```python
import jax
import jax.numpy as jnp
from jax import lax
from jax.sharding import PartitionSpec as P

ROW_BLOCKS = 12


def fdot(left, right):
    return jnp.dot(left, right, precision=lax.Precision.HIGHEST, preferred_element_type=jnp.float32)


def shards(blocks, block_ids, counts):
    n_row = lax.axis_size("row")
    n_col = lax.axis_size("col")
    n_layer = lax.axis_size("layer")
    listed = blocks.shape[3]
    side = blocks.shape[-1]
    nblk = ROW_BLOCKS * n_row
    cblk = nblk // n_col
    row_init = jnp.zeros((ROW_BLOCKS, side, nblk, side), jnp.float32)
    values = lax.all_gather(blocks, "col", axis=1, tiled=True)
    slots = lax.all_gather(block_ids, "col", axis=1, tiled=True)
    live = lax.all_gather(counts, "col", axis=1, tiled=True)
    number = values.shape[1]
    slots = slots.reshape(number, listed)
    position = lax.broadcasted_iota(jnp.int32, (number, listed), 1)
    alive = position < live.reshape(number, 1)
    tiles = lax.broadcasted_iota(jnp.int32, (number, listed), 0)
    local_row = slots // cblk
    glob_col = tiles * cblk + slots % cblk
    values = jnp.where(
        alive[:, :, None, None], values.reshape(number, listed, side, side), jnp.float32(0.0)
    )
    row_panel = row_init.at[local_row.reshape(-1), :, glob_col.reshape(-1), :].add(
        values.reshape(-1, side, side)
    )
    col_init = jnp.zeros((nblk, side, cblk, side), jnp.float32)
    values = lax.all_gather(
        blocks.reshape(1, listed, side, side), ("row", "layer"), axis=0, tiled=True
    )
    slots = lax.all_gather(block_ids.reshape(1, listed), ("row", "layer"), axis=0, tiled=True)
    live = lax.all_gather(counts.reshape(1), ("row", "layer"), axis=0, tiled=True)
    number = values.shape[0]
    position = lax.broadcasted_iota(jnp.int32, (number, listed), 1)
    alive = position < live.reshape(number, 1)
    owner = lax.broadcasted_iota(jnp.int32, (number, listed), 0)
    glob_row = owner // n_layer * ROW_BLOCKS + slots // cblk
    local_col = slots % cblk
    values = jnp.where(alive[:, :, None, None], values, jnp.float32(0.0))
    col_panel = col_init.at[glob_row.reshape(-1), :, local_col.reshape(-1), :].add(
        values.reshape(-1, side, side)
    )
    row_flat = row_panel.reshape(ROW_BLOCKS * side, nblk * side)
    col_flat = col_panel.reshape(nblk * side, cblk * side)
    square = lax.psum_scatter(fdot(row_flat, col_flat), "layer", scatter_dimension=0, tiled=True)
    cubed = fdot(lax.all_gather(square, "col", axis=1, tiled=True), col_flat)
    return 3.0 * square - 2.0 * cubed


def solution(mesh):
    return jax.shard_map(
        shards,
        mesh=mesh,
        in_specs=(
            P("row", "col", "layer", None, None, None),
            P("row", "col", "layer", None),
            P("row", "col", "layer"),
        ),
        out_specs=P(("row", "layer"), "col"),
        check_vma=False,
    )
```

profile of v0, /device:TPU:1, one launch (start us, length us, event | category | flops | bytes accessed | tf_op | source)
XLA Modules:
  0.0 843.6 jit_solution(12151336246089383153)
XLA Ops:
  6.5 0.7 all-gather.7.cloned.1.call-update
  7.3 0.7 all-gather.11.cloned.1.call-update
  8.7 1.3 dynamic-slice.1
  10.0 1.2 dynamic-slice
  11.2 0.6 bitcast_dynamic-update-slice_fusion
  11.9 0.7 bitcast_dynamic-update-slice_fusion.1
  12.5 7.3 all-reduce.1
  19.9 7.0 all-reduce
  26.8 7.8 all_gather.21
  34.7 0.1 lt.87
  35.3 14.2 %all-gather = s32[8,1,1,8]{3,2,1,0:T(1,128)S(1)} all-gather(s32[1,1,1,8]{3,2,1,0:T(1,128)} %param.4), channel_id=2, replica_groups=mesh['row'=4,'col'=4,'layer'=2] {'row','layer'}, dimensions={0}, use_global_device_ids=true | all-gather | bytes 288 | tf_op jit(solution)/shard_map/all_gather | solution.py:42
  49.9 7.3 all-gather.7.cloned.1.call-done
  57.2 1.8 bitcast_select_fusion.1
  59.0 12.6 %broadcast_in_dim.36 = f32[12,128,48,128]{3,1,2,0:T(8,128)} broadcast(f32[]{:T(128)} %constant.53.clone.1), dimensions={} | broadcast | bytes 37748740 | tf_op jit(solution)/shard_map/broadcast_in_dim | solution.py:21
  71.5 6.5 scatter_fusion
  78.0 35.6 %copy.17 = f32[12,128,48,128]{3,2,1,0:T(8,128)} copy(f32[12,128,48,128]{3,1,2,0:T(8,128)} %scatter_fusion) | data formatting | bytes 75497472 | tf_op jit(solution)/shard_map/scatter-add | solution.py:35
  113.6 4.5 bitcast_select_fusion
  118.2 12.6 %broadcast_in_dim.39 = f32[48,128,12,128]{3,1,2,0:T(8,128)} broadcast(f32[]{:T(128)} %constant.53.clone.1), dimensions={} | broadcast | bytes 37748740 | tf_op jit(solution)/shard_map/broadcast_in_dim | solution.py:38
  130.7 14.1 %scatter_fusion.1 = f32[48,128,12,128]{3,1,2,0:T(8,128)} fusion(f32[48,128,12,128]{3,1,2,0:T(8,128)} %broadcast_in_dim.39, s32[64]{0:T(128)S(1)} %fusion.17, f32[64,128,128]{2,1,0:T(8,128)} %bitcast.59), kind=kCustom, calls=%fused_computation.1 | custom fusion | flops 1048576 | bytes 12583424 | tf_op jit(solution)/shard_map/scatter-add | solution.py:51
  144.8 36.9 %copy.21 = f32[48,128,12,128]{1,0,3,2:T(8,128)} copy(f32[48,128,12,128]{3,1,2,0:T(8,128)} %scatter_fusion.1) | data formatting | bytes 75497472 | tf_op jit(solution)/shard_map/scatter-add | solution.py:51
  181.7 210.7 %fusion.2 = f32[1536,1536]{1,0:T(8,128)} fusion(f32[192,8,48,128]{3,2,1,0:T(8,128)} %bitcast.58, f32[192,8,48,128]{3,2,1,0:T(8,128)} %bitcast.56), kind=kOutput, calls=%fused_computation.4 | convolution fusion | flops 173946175488 | bytes 84934656 | tf_op jit(solution)/shard_map/dot_general | solution.py:10
  392.5 17.0 %reduce-scatter.2.cloned.1.call-done = f32[768,1536]{1,0:T(8,128)} async-done(((f32[1536,1536]{1,0:T(8,128)}), f32[768,1536]{1,0:T(8,128)}) %reduce-scatter.2.cloned.1.call-update) | async-done | bytes 4718608 | tf_op jit(solution)/shard_map/reduce_scatter | solution.py:56
  409.6 324.9 %all-gather.9.cloned.1.call-done = f32[768,6144]{1,0:T(8,128)} async-done(((f32[768,1536]{1,0:T(8,128)}), f32[768,6144]{1,0:T(8,128)}) %all-gather.9.cloned.1.call-update) | async-done | bytes 18874384 | tf_op jit(solution)/shard_map/all_gather | solution.py:57
  734.5 102.6 %multiply_subtract_fusion = f32[768,1536]{1,0:T(8,128)} fusion(f32[768,1536]{1,0:T(8,128)} %reduce-scatter.2.cloned.1.call-done, f32[768,6144]{1,0:T(8,128)} %all-gather.9.cloned.1.call-done, f32[192,8,48,128]{3,2,1,0:T(8,128)} %bitcast.57), kind=kOutput, calls=%fused_computation.10 | convolution fusion | flops 86976626688 | bytes 66060288 | tf_op jit(solution)/shard_map/dot_general | solution.py:10
  (26 shorter events, 1.0 us)
Async XLA Ops:
  6.5 50.6 %all-gather.7.cloned.1.call-start = ((), (), s32[]{:S(2)}) async-start(), calls=%async_computation.1 | async-start | bytes 2621440 | tf_op jit(solution)/shard_map/all_gather | solution.py:22
  7.3 106.4 %all-gather.11.cloned.1.call-start = ((), (), s32[]{:S(2)}) async-start(), calls=%async_computation.4 | async-start | bytes 4718592 | tf_op jit(solution)/shard_map/all_gather | solution.py:39
  8.0 401.6 %reduce-scatter.2.cloned.1.call-start = ((), (), s32[]{:S(2)}) async-start(), calls=%async_computation.2 | async-start | bytes 14155776 | tf_op jit(solution)/shard_map/reduce_scatter | solution.py:56
  392.5 342.0 %all-gather.9.cloned.1.call-start = ((), (), s32[]{:S(2)}) async-start(), calls=%async_computation.3 | async-start | bytes 23592960 | tf_op jit(solution)/shard_map/all_gather | solution.py:57
Sparse Core Ops, SparseCore 0:
  8.9 48.1 all-gather.6
  59.1 35.8 all-gather.10
  392.6 16.9 reduce-scatter.1
  411.0 323.4 all-gather.8
where the time goes:
time: 846 us; the launch traced here: 844 us
  waiting for transfers between devices  351 us (41%)
  matrix products  313 us (37%)
  local copies, waits for them, and re-layouts  102 us (12%)
  blocking collectives  36.4 us (4%)
  other arithmetic  27.2 us (3%)
  between operations  13.8 us (2%)
    all_gather x1, waiting for transfers between devices, shards(): cubed = fdot(lax.all_gather(square, 'col', axis=1, tiled=True), col_flat)  325 us
    dot_general x2, matrix products, fdot(): jnp.dot(left, right, precision=lax.Precision.HIGHEST, preferred_element_t...  313 us
    scatter-add x1, local copies, waits for them, and re-layouts, shards(): col_init.at[glob_row.reshape(-1), :, local_col.reshape(-1), :]  36.9 us
    scatter-add x1, local copies, waits for them, and re-layouts, shards(): row_init.at[local_row.reshape(-1), :, glob_col.reshape(-1), :]  35.6 us
    reduce_scatter x1, waiting for transfers between devices, shards(): lax.psum_scatter(fdot(row_flat, col_flat), 'layer', scatter_dimension=0,...  17 us
  transfers between devices with their start and end apart: 4, of which 3 were waited for; matrix products, arithmetic and copies ran while one was open for 7% of the time, Pallas kernels for 0%

commit v1 on v0

v1 whole, which is shorter than its diff:
```python
import functools

import jax
import jax.numpy as jnp
from jax import lax
from jax.experimental import pallas as pl
from jax.experimental.pallas import tpu as pltpu
from jax.sharding import PartitionSpec as P

ROW_BLOCKS = 12
DEPTH = 4
GROUP = 4
AXES = ("row", "col", "layer")


def split(x):
    high = x.astype(jnp.bfloat16)
    low = (x - high.astype(jnp.float32)).astype(jnp.bfloat16)
    return high, low


def kernel(
    sizes,
    where_ref,
    meta_ref,
    blocks_ref,
    out_ref,
    buffer,
    sem,
    left,
    right,
    panel,
    square,
    wide,
    head,
    nxt,
    left_row,
    chead,
    cnext,
    ccol,
    plan,
):
    n_row, n_col, n_layer, listed, side = sizes
    nblk = ROW_BLOCKS * n_row
    cblk = nblk // n_col
    half = ROW_BLOCKS // n_layer
    rows = half * side
    per_row = n_col * n_layer
    chunks = n_row * per_row
    my_row, my_col, my_layer = where_ref[0], where_ref[1], where_ref[2]

    def fetch(chunk, slot):
        return pltpu.make_async_copy(
            blocks_ref.at[pl.ds(chunk * listed, listed)], buffer.at[slot], sem.at[slot]
        )

    def clear(i, _):
        head[i] = -1
        chead[i] = -1
        return 0

    lax.fori_loop(0, nblk, clear, 0)
    base = my_row * per_row
    for d in range(DEPTH):
        fetch(base + d, d).start()

    def load_left(t, count):
        slot = lax.rem(t, DEPTH)
        chunk = base + t
        fetch(chunk, slot).wait()
        col = t // n_layer

        def one(s, count):
            ident = meta_ref[chunk, s]
            row = ident // cblk - my_layer * half
            use = (s < meta_ref[chunk, listed]) & (row >= 0) & (row < half)

            @pl.when(use)
            def _():
                k = col * cblk + lax.rem(ident, cblk)
                nxt[count] = head[k]
                head[k] = count
                left_row[count] = row
                high, low = split(buffer[slot, s])
                left[count, :, :side] = high
                left[count, :, side:] = low

            return count + use.astype(jnp.int32)

        count = lax.fori_loop(0, listed, one, count)

        @pl.when(t + DEPTH < per_row)
        def _():
            fetch(chunk + DEPTH, slot).start()

        return count

    lax.fori_loop(0, per_row, load_left, 0)

    for d in range(DEPTH):
        fetch(d, d).start()

    def zero(j, _):
        square[j] = jnp.zeros((rows, side), jnp.float32)
        return 0

    lax.fori_loop(0, nblk, zero, 0)
    for s in range(listed):
        right[s, side:, side:] = jnp.zeros((side, side), jnp.bfloat16)

    def stream(t, ccount):
        slot = lax.rem(t, DEPTH)
        row0 = t // per_row * ROW_BLOCKS
        col = lax.rem(t, per_row) // n_layer
        live = meta_ref[t, listed]
        fetch(t, slot).wait()

        def one(s, carry):
            count, ccount = carry
            ident = meta_ref[t, s]
            k = row0 + ident // cblk
            local = lax.rem(ident, cblk)
            alive = s < live
            mine = alive & (col == my_col)

            @pl.when(alive & ((head[k] >= 0) | mine))
            def _():
                high, low = split(buffer[slot, s])
                right[s, :side, :side] = high
                right[s, side:, :side] = high
                right[s, :side, side:] = low

            @pl.when(mine)
            def _():
                panel[ccount] = right[s]
                cnext[ccount] = chead[k]
                chead[k] = ccount
                ccol[ccount] = local

            def more(carry):
                return carry[0] >= 0

            def add(carry):
                a, count = carry
                plan[0, count] = a
                plan[1, count] = s
                plan[2, count] = col * cblk + local
                plan[3, count] = left_row[a]
                return nxt[a], count + 1

            first = jnp.where(alive, head[k], -1)
            _, count = lax.while_loop(more, add, (first, count))
            return count, ccount + mine.astype(jnp.int32)

        count, ccount = lax.fori_loop(0, listed, one, (0, ccount))

        @pl.when(t + DEPTH < chunks)
        def _():
            fetch(t + DEPTH, slot).start()

        for u in range(GROUP - 1):
            plan[0, count + u] = 0
            plan[1, count + u] = 0
            plan[2, count + u] = nblk
            plan[3, count + u] = 0

        def group(g, _):
            parts = []
            for u in range(GROUP):
                e = g * GROUP + u
                parts.append(
                    jnp.dot(
                        left[plan[0, e]], right[plan[1, e]], preferred_element_type=jnp.float32
                    )
                )
            for u in range(GROUP):
                e = g * GROUP + u
                at = pl.ds(pl.multiple_of(plan[3, e] * side, side), side)
                j = plan[2, e]
                square[j, at, :] = square[j, at, :] + (parts[u][:, :side] + parts[u][:, side:])
            return 0

        lax.fori_loop(0, (count + GROUP - 1) // GROUP, group, 0)
        return ccount

    lax.fori_loop(0, chunks, stream, 0)

    def first(j, _):
        at = pl.ds(pl.multiple_of(j * side, side), side)
        out_ref[:, at] = 3.0 * square[my_col * cblk + j]
        return 0

    lax.fori_loop(0, cblk, first, 0)

    def cube(k, _):
        @pl.when(chead[k] >= 0)
        def _():
            high, low = split(-2.0 * square[k])
            wide[:, :side] = high
            wide[:, side:] = low

            def more(c):
                return c >= 0

            def add(c):
                at = pl.ds(pl.multiple_of(ccol[c] * side, side), side)
                part = jnp.dot(wide[...], panel[c], preferred_element_type=jnp.float32)
                out_ref[:, at] = out_ref[:, at] + (part[:, :side] + part[:, side:])
                return cnext[c]

            lax.while_loop(more, add, chead[k])

        return 0

    lax.fori_loop(0, nblk, cube, 0)


def purify(sizes, where, meta, blocks):
    n_row, n_col, n_layer, listed, side = sizes
    nblk = ROW_BLOCKS * n_row
    cblk = nblk // n_col
    half = ROW_BLOCKS // n_layer
    rows = half * side
    lefts = min(n_col * n_layer * listed, half * nblk)
    mids = n_row * n_layer * listed
    return pl.pallas_call(
        functools.partial(kernel, sizes),
        out_shape=jax.ShapeDtypeStruct((rows, cblk * side), jnp.float32),
        in_specs=[
            pl.BlockSpec(memory_space=pltpu.SMEM),
            pl.BlockSpec(memory_space=pltpu.SMEM),
            pl.BlockSpec(memory_space=pl.ANY),
        ],
        out_specs=pl.BlockSpec(memory_space=pltpu.VMEM),
        scratch_shapes=[
            pltpu.VMEM((DEPTH, listed, side, side), jnp.float32),
            pltpu.SemaphoreType.DMA((DEPTH,)),
            pltpu.VMEM((lefts, side, 2 * side), jnp.bfloat16),
            pltpu.VMEM((listed, 2 * side, 2 * side), jnp.bfloat16),
            pltpu.VMEM((mids, 2 * side, 2 * side), jnp.bfloat16),
            pltpu.VMEM((nblk + 1, rows, side), jnp.float32),
            pltpu.VMEM((rows, 2 * side), jnp.bfloat16),
            pltpu.SMEM((nblk,), jnp.int32),
            pltpu.SMEM((lefts,), jnp.int32),
            pltpu.SMEM((lefts,), jnp.int32),
            pltpu.SMEM((nblk,), jnp.int32),
            pltpu.SMEM((mids,), jnp.int32),
            pltpu.SMEM((mids,), jnp.int32),
            pltpu.SMEM((4, listed * half + GROUP), jnp.int32),
        ],
        compiler_params=pltpu.CompilerParams(vmem_limit_bytes=62 * 1024 * 1024),
    )(where, meta, blocks)


def shards(blocks, block_ids, counts):
    n_row, n_col, n_layer = (lax.axis_size(a) for a in AXES)
    listed, side = blocks.shape[3], blocks.shape[-1]
    own = jnp.concatenate([block_ids.reshape(1, listed), counts.reshape(1, 1)], axis=1)
    meta = lax.all_gather(own, AXES, axis=0, tiled=True)
    values = lax.all_gather(blocks.reshape(listed, side, side), AXES, axis=0, tiled=True)
    where = jnp.stack([lax.axis_index(a) for a in AXES]).astype(jnp.int32)
    return purify((n_row, n_col, n_layer, listed, side), where, meta, values)


def solution(mesh):
    return jax.shard_map(
        shards,
        mesh=mesh,
        in_specs=(
            P("row", "col", "layer", None, None, None),
            P("row", "col", "layer", None),
            P("row", "col", "layer"),
        ),
        out_specs=P(("row", "layer"), "col"),
        check_vma=False,
    )
```

time: 846 us -> 188 us (0.22)
  matrix products: 313 us -> 0 us
  waiting for transfers between devices: 351 us -> 74.8 us
  local copies, waits for them, and re-layouts: 102 us -> 0 us
  Pallas kernels: 0 us -> 50.7 us
  other arithmetic: 27.2 us -> 1.39 us
    dot_general x2 -> x0, matrix products: 313 us -> none  [fdot(): jnp.dot(left, right, precision=lax.Precision.HIGHEST, preferred_element_t...]
    all_gather x3 -> x1, waiting for transfers between devices: 332 us -> 74.1 us  [shards(): lax.all_gather(blocks.reshape(listed, side, side), AXES, axis=0, tiled=True)]
    scatter-add x2 -> x0, local copies, waits for them, and re-layouts: 72.5 us -> none  [the longest x1 36.9 us: shards(): col_init.at[glob_row.reshape(-1), :, local_col.reshape(-1), :]]
    pallas_call x0 -> x1, Pallas kernels: none -> 50.7 us  [purify(): pl.pallas_call(functools.partial(kernel, sizes), out_shape=jax.ShapeDtype...]
    broadcast_in_dim x2 -> x0, local copies, waits for them, and re-layouts: 25.2 us -> none  [the longest x1 12.6 us: shards(): col_init = jnp.zeros((nblk, side, cblk, side), jnp.float32)]
    all_gather x2 -> x1, blocking collectives: 22.1 us -> 44.4 us  [shards(): meta = lax.all_gather(own, AXES, axis=0, tiled=True)]
    scatter-add x2 -> x0, other arithmetic: 20.6 us -> none  [the longest x1 14.1 us: shards(): col_init.at[glob_row.reshape(-1), :, local_col.reshape(-1), :]]
    reduce_scatter x1 -> x0, waiting for transfers between devices: 17 us -> none  [shards(): lax.psum_scatter(fdot(row_flat, col_flat), 'layer', scatter_dimension=0,...]
  transfers between devices with their start and end apart: 4 -> 1, of which waited for: 3 -> 1; matrix products, arithmetic and copies ran while one was open for 7% -> 1% of each run, Pallas kernels for 0% -> 0%
where the time goes in v1:
time: 188 us; the launch traced here: 185 us
  waiting for transfers between devices  74.8 us (40%)
  Pallas kernels  50.7 us (27%)
  blocking collectives  44.4 us (24%)
  between operations  14.1 us (8%)
    all_gather x1, waiting for transfers between devices, shards(): lax.all_gather(blocks.reshape(listed, side, side), AXES, axis=0, tiled=True)  74.1 us
    pallas_call x1, Pallas kernels, purify(): pl.pallas_call(functools.partial(kernel, sizes), out_shape=jax.ShapeDtype...  50.7 us
    all_gather x1, blocking collectives, shards(): meta = lax.all_gather(own, AXES, axis=0, tiled=True)  44.4 us
  transfers between devices with their start and end apart: 1, of which 1 were waited for; matrix products, arithmetic and copies ran while one was open for 1% of the time, Pallas kernels for 0%

profile of v1, /device:TPU:1, one launch (start us, length us, event | category | flops | bytes accessed | tf_op | source)
XLA Modules:
  0.0 185.4 jit_solution(5173736904169615520)
XLA Ops:
  6.5 0.0 all-gather.4.cloned.1.call-start
  6.5 0.7 all-gather.4.cloned.1.call-update
  7.9 0.7 add_bitcast_fusion
  8.6 44.4 %all-gather.1 = s32[32,1,9]{2,1,0:T(1,128)} all-gather(s32[1,1,9]{2,1,0:T(1,128)S(1)} %add_bitcast_fusion), channel_id=1, replica_groups=mesh['row'=4,'col'=4,'layer'=2] {'row','col','layer'}, dimensions={0}, use_global_device_ids=true | all-gather | bytes 1188 | tf_op jit(solution)/shard_map/all_gather | solution.py:259
  53.1 0.7 pad_add_fusion.where_ref
  53.7 74.1 %all-gather.4.cloned.1.call-done = f32[1,1,1,256,128,128]{5,4,2,1,0,3:T(8,128)} async-done(((f32[1,1,1,8,128,128]{5,4,2,1,0,3:T(8,128)}), f32[1,1,1,256,128,128]{5,4,2,1,0,3:T(8,128)}) %all-gather.4.cloned.1.call-update) | async-done | bytes 16777232 | tf_op jit(solution)/shard_map/all_gather | solution.py:260
  127.8 50.7 %shard_map.37 = f32[768,1536]{1,0:T(8,128)} custom-call(s32[3]{0:T(128)} %pad_add_fusion.where_ref, s32[32,9]{1,0:T(8,128)} %bitcast.13, f32[256,128,128]{2,1,0:T(8,128)} %bitcast.11), custom_call_target="tpu_custom_call" | custom-call | tf_op jit(solution)/shard_map/pallas_call | solution.py:226
Async XLA Ops:
  6.5 121.3 %all-gather.4.cloned.1.call-start = ((), (), s32[]{:S(2)}) async-start(), calls=%async_computation | async-start | bytes 17301504 | tf_op jit(solution)/shard_map/all_gather | solution.py:260
Sparse Core Ops, SparseCore 0:
  10.4 117.4 all-gather.3

commit v2 on v0

v2 whole, which is shorter than its diff:
```python
import functools

import jax
import jax.numpy as jnp
from jax import lax
from jax.experimental import pallas as pl
from jax.experimental.pallas import tpu as pltpu
from jax.sharding import PartitionSpec as P

ROW_BLOCKS = 12
GROUP = 4
CHUNK = 768
PANEL_MB = 16
TILE_MB = 40
AXES = ("row", "col", "layer")
VMEM = pl.BlockSpec(memory_space=pltpu.VMEM)
SMEM = pl.BlockSpec(memory_space=pltpu.SMEM)
HBM = pl.BlockSpec(memory_space=pltpu.HBM)


def params(megabytes):
    return pltpu.CompilerParams(vmem_limit_bytes=megabytes * 1024 * 1024)


def split(x):
    high = x.astype(jnp.bfloat16)
    low = (x - high.astype(jnp.float32)).astype(jnp.bfloat16)
    return high, low


def product(left, right):
    part = jnp.dot(
        left, jnp.concatenate([right, right], axis=0), preferred_element_type=jnp.float32
    )
    side = right.shape[0]
    return part[:, :side] + part[:, side:]


def lanes(i, side):
    return pl.ds(pl.multiple_of(i * side, side), side)


def start_copies(side, listed, array_refs, buffer, lists, sem):
    out = []
    for i, ref in enumerate(array_refs):
        value = pltpu.make_async_copy(
            ref.at[pl.ds(0, listed * side)],
            buffer.at[pl.ds(i * listed * side, listed * side)],
            sem.at[0, i],
        )
        names = pltpu.make_async_copy(
            ref.at[pl.ds(listed * side, 8)], lists.at[pl.ds(i * 8, 8)], sem.at[1, i]
        )
        value.start()
        names.start()
        out.append((value, names))
    return out


def tile_row(segment, my_row, my_layer, n_layer):
    first, second, _, other = segment
    layer = (n_layer - 1 - my_layer) if other else my_layer
    return my_row ^ jnp.where(layer == 0, first, second)


def panel_kernel(sizes, kind, segments, where_ref, *refs):
    n_row, n_col, n_layer, listed, side = sizes
    arrays = len(segments)
    array_refs = refs[:arrays]
    panel, head, nxt, tag, buffer, lists, sem = refs[arrays:]
    nblk = ROW_BLOCKS * n_row
    cblk = nblk // n_col
    half = ROW_BLOCKS // n_layer
    my_row, my_col, my_layer = where_ref[0], where_ref[1], where_ref[2]
    moves = start_copies(side, listed, array_refs, buffer, lists, sem)

    def clear(i, _):
        head[i] = -1
        return 0

    lax.fori_loop(0, nblk, clear, 0)
    count = jnp.int32(0)
    for i, (value, names) in enumerate(moves):
        value.wait()
        names.wait()
        row = tile_row(segments[i], my_row, my_layer, n_layer)
        col = lax.rem(my_col + (n_col - segments[i][2]), n_col)
        live = lists[i * 8, listed].astype(jnp.int32)

        def one(s, count, i=i, row=row, col=col, live=live):
            ident = lists[i * 8, s].astype(jnp.int32)
            line = ident // cblk
            local = lax.rem(ident, cblk)
            if kind == "left":
                key, mark = col * cblk + local, line - my_layer * half
                use = (s < live) & (mark >= 0) & (mark < half)
            else:
                key, mark = row * ROW_BLOCKS + line, local
                use = s < live

            @pl.when(use)
            def _():
                nxt[count] = head[key]
                head[key] = count
                tag[count] = mark
                high, low = split(buffer[lanes(i * listed + s, side), :])
                panel[count, :, :side] = high
                panel[count, :, side:] = low

            return count + use.astype(jnp.int32)

        count = lax.fori_loop(0, listed, one, count)


def panel_call(sizes, kind, segments, arrays, most, where):
    n_row, n_col, n_layer, listed, side = sizes
    nblk = ROW_BLOCKS * n_row
    total = len(segments) * listed
    return pl.pallas_call(
        functools.partial(panel_kernel, sizes, kind, segments),
        out_shape=[
            jax.ShapeDtypeStruct((most, side, 2 * side), jnp.bfloat16),
            jax.ShapeDtypeStruct((nblk,), jnp.int32),
            jax.ShapeDtypeStruct((most,), jnp.int32),
            jax.ShapeDtypeStruct((most,), jnp.int32),
        ],
        in_specs=[SMEM] + [HBM] * len(arrays),
        out_specs=[VMEM, SMEM, SMEM, SMEM],
        scratch_shapes=[
            pltpu.VMEM((total * side, side), jnp.float32),
            pltpu.SMEM((len(segments) * 8, side), jnp.float32),
            pltpu.SemaphoreType.DMA((2, len(segments))),
        ],
        compiler_params=params(PANEL_MB),
        name=kind + "_panel",
    )(where, *arrays)


def tile_kernel(sizes, shifts, segments, *refs):
    n_row, n_col, n_layer, listed, side = sizes
    arrays = len(segments)
    where_ref, head, nxt, left_row, chead, cnext, ccol, left_ref, panel_ref = refs[:9]
    array_refs = refs[9 : 9 + arrays]
    rest = refs[9 + arrays :]
    if shifts[0]:
        before, rest = rest[0], rest[1:]
    out_ref, buffer, lists, sem, left, panel, late, right, square, wide, plan = rest
    nblk = ROW_BLOCKS * n_row
    cblk = nblk // n_col
    rows = ROW_BLOCKS // n_layer * side
    my_row, my_col, my_layer = where_ref[0], where_ref[1], where_ref[2]
    moves = start_copies(side, listed, array_refs, buffer, lists, sem)
    get_left = pltpu.make_async_copy(left_ref, left, late.at[0])
    get_panel = pltpu.make_async_copy(panel_ref, panel, late.at[1])
    get_left.start()
    get_panel.start()
    if shifts[0]:
        get_before = pltpu.make_async_copy(before, out_ref, late.at[2])
        get_before.start()
    for tile_shift in shifts:
        col = lax.rem(my_col + (n_col - tile_shift), n_col)

        def zero(j, _):
            square[j] = jnp.zeros((rows, side), jnp.float32)
            return 0

        lax.fori_loop(0, cblk, zero, 0)
        count = jnp.int32(0)
        for i, (value, names) in enumerate(moves):
            if segments[i][2] != tile_shift:
                continue
            value.wait()
            names.wait()
            row = tile_row(segments[i], my_row, my_layer, n_layer)
            live = lists[i * 8, listed].astype(jnp.int32)

            def one(s, count, i=i, row=row, live=live):
                ident = lists[i * 8, s].astype(jnp.int32)
                at = i * listed + s
                k = row * ROW_BLOCKS + ident // cblk
                local = lax.rem(ident, cblk)
                first = jnp.where(s < live, head[k], -1)

                @pl.when(first >= 0)
                def _():
                    high, low = split(buffer[lanes(at, side), :])
                    right[at, :, :side] = high
                    right[at, :, side:] = low

                def more(carry):
                    return carry[0] >= 0

                def add(carry):
                    a, count = carry
                    plan[0, count] = a
                    plan[1, count] = at
                    plan[2, count] = local
                    plan[3, count] = left_row[a]
                    return nxt[a], count + 1

                return lax.while_loop(more, add, (first, count))[1]

            count = lax.fori_loop(0, listed, one, count)

        for u in range(GROUP - 1):
            plan[0, count + u] = 0
            plan[1, count + u] = 0
            plan[2, count + u] = cblk
            plan[3, count + u] = 0

        def group(g, _):
            parts = []
            for u in range(GROUP):
                e = g * GROUP + u
                parts.append(product(left[plan[0, e]], right[plan[1, e]]))
            for u in range(GROUP):
                e = g * GROUP + u
                at = lanes(plan[3, e], side)
                j = plan[2, e]
                square[j, at, :] = square[j, at, :] + parts[u]
            return 0

        if tile_shift == shifts[0]:
            get_left.wait()
        lax.fori_loop(0, (count + GROUP - 1) // GROUP, group, 0)
        if tile_shift == shifts[0]:
            get_panel.wait()
            if tile_shift:
                get_before.wait()
        if not tile_shift:

            def begin(j, _):
                out_ref[:, lanes(j, side)] = 3.0 * square[j]
                return 0

            lax.fori_loop(0, cblk, begin, 0)

        def cube(j, _, col=col):
            k = col * cblk + j

            @pl.when(chead[k] >= 0)
            def _():
                high, low = split(-2.0 * square[j])
                wide[:, :side] = high
                wide[:, side:] = low

                def more(c):
                    return c >= 0

                def add(c):
                    at = lanes(ccol[c], side)
                    for m in range(0, rows, CHUNK):
                        line = pl.ds(m, CHUNK)
                        out_ref[line, at] = out_ref[line, at] + product(wide[line, :], panel[c])
                    return cnext[c]

                lax.while_loop(more, add, chead[k])

            return 0

        lax.fori_loop(0, cblk, cube, 0)


def tile_call(sizes, shifts, segments, arrays, where, lefts, rights, before):
    n_row, n_col, n_layer, listed, side = sizes
    nblk = ROW_BLOCKS * n_row
    cblk = nblk // n_col
    half = ROW_BLOCKS // n_layer
    rows = half * side
    total = len(segments) * listed
    left, head, nxt, left_row = lefts
    panel, chead, cnext, ccol = rights
    extra = [] if before is None else [before]
    return pl.pallas_call(
        functools.partial(tile_kernel, sizes, shifts, segments),
        out_shape=jax.ShapeDtypeStruct((rows, cblk * side), jnp.float32),
        in_specs=[SMEM] * 7 + [HBM] * (2 + len(arrays) + len(extra)),
        out_specs=VMEM,
        scratch_shapes=[
            pltpu.VMEM((total * side, side), jnp.float32),
            pltpu.SMEM((len(segments) * 8, side), jnp.float32),
            pltpu.SemaphoreType.DMA((2, len(segments))),
            pltpu.VMEM(left.shape, left.dtype),
            pltpu.VMEM(panel.shape, panel.dtype),
            pltpu.SemaphoreType.DMA((3,)),
            pltpu.VMEM((total, side, 2 * side), jnp.bfloat16),
            pltpu.VMEM((cblk + 1, rows, side), jnp.float32),
            pltpu.VMEM((rows, 2 * side), jnp.bfloat16),
            pltpu.SMEM((4, total * half + GROUP), jnp.int32),
        ],
        compiler_params=params(TILE_MB),
        name="tiles_" + "_".join(str(s) for s in shifts),
    )(where, head, nxt, left_row, chead, cnext, ccol, left, panel, *arrays, *extra)


def shards(blocks, block_ids, counts):
    n_row, n_col, n_layer = (lax.axis_size(a) for a in AXES)
    listed, side = blocks.shape[3], blocks.shape[-1]
    sizes = (n_row, n_col, n_layer, listed, side)
    half = ROW_BLOCKS // n_layer

    def flip(bits):
        pairs = []
        for r in range(n_row):
            for k in range(n_layer):
                pairs.append((r * n_layer + k, (r ^ bits[min(k, 1)]) * n_layer + k))
        return lambda y: lax.ppermute(y, ("row", "layer"), pairs)

    across, along = flip((1, 2)), flip((2, 1))

    def ring(y):
        return lax.ppermute(y, "col", [(i, (i + 1) % n_col) for i in range(n_col)])

    def sibling(y):
        return lax.ppermute(y, "layer", [(i, n_layer - 1 - i) for i in range(n_layer)])

    where = jnp.stack([lax.axis_index(a) for a in AXES]).astype(jnp.int32)
    names = jnp.concatenate([block_ids.reshape(listed), counts.reshape(1)]).astype(jnp.float32)
    names = jnp.pad(names.reshape(1, listed + 1), ((0, 7), (0, side - listed - 1)))
    own = jnp.concatenate([blocks.reshape(listed * side, side), names], axis=0)

    ways = {"A": (0, 0), "U": (1, 2), "V": (2, 1), "D": (3, 3)}
    held = {("A", 0): own}
    twin = {}
    lefts = rights = total = None
    fresh = [("A", 0)]

    def gathered(names):
        segments = [(*ways[k], s, other) for other in (False, True) for k, s in names]
        return segments, [source[name] for source in (held, twin) for name in names]

    def quads(shifts):
        return [(k, s) for s in shifts for k in ways]

    def tiles(shifts, total):
        for i in range(0, len(shifts), 2):
            segments, arrays = gathered(quads(shifts[i : i + 2]))
            total = tile_call(
                sizes, shifts[i : i + 2], segments, arrays, where, lefts, rights, total
            )
        return total

    for t in range(n_col + 2):
        sent = {}
        if t < n_col:
            sent[("U", t)] = across(held[("A", t)])
            sent[("V", t)] = along(held[("A", t)])
        if t < n_col - 1:
            sent[("A", t + 1)] = ring(held[("A", t)])
        if 1 <= t <= n_col:
            sent[("D", t - 1)] = along(held[("U", t - 1)])
        copied = {name: sibling(held[name]) for name in fresh}
        twin.update(copied)
        if t == 2:
            segments, arrays = gathered(quads([0]))
            most = n_row * n_layer * listed
            rights = panel_call(sizes, "right", segments, arrays, most, where)
        if t == n_col - 1:
            segments, arrays = gathered([("A", s) for s in range(n_col)])
            most = min(n_col * n_layer * listed, half * ROW_BLOCKS * n_row)
            lefts = panel_call(sizes, "left", segments, arrays, most, where)
            total = tiles(list(range(n_col - 3)), total)
        if t == n_col:
            total = tiles(list(range(n_col - 3, n_col - 1)), total)
        if t == n_col + 1:
            return tiles([n_col - 1], total)
        kept = lax.optimization_barrier((sent, copied, rights, lefts, total))
        sent, copied, rights, lefts, total = kept
        held.update(sent)
        twin.update(copied)
        fresh = list(sent)


def solution(mesh):
    return jax.shard_map(
        shards,
        mesh=mesh,
        in_specs=(
            P("row", "col", "layer", None, None, None),
            P("row", "col", "layer", None),
            P("row", "col", "layer"),
        ),
        out_specs=P(("row", "layer"), "col"),
        check_vma=False,
    )
```

time: 846 us -> 130 us (0.15)
  waiting for transfers between devices: 351 us -> 37.2 us
  matrix products: 313 us -> 0 us
  local copies, waits for them, and re-layouts: 102 us -> 13.5 us
  Pallas kernels: 0 us -> 55.3 us
  blocking collectives: 36.4 us -> 0 us
  other arithmetic: 27.2 us -> 1.88 us
  starting transfers between devices: 0.12 us -> 20.3 us
  between operations: 13.8 us -> 0.93 us
    all_gather x3 -> x0, waiting for transfers between devices: 332 us -> none  [the longest x1 325 us: shards(): cubed = fdot(lax.all_gather(square, 'col', axis=1, tiled=True), col_flat)]
    dot_general x2 -> x0, matrix products: 313 us -> none  [fdot(): jnp.dot(left, right, precision=lax.Precision.HIGHEST, preferred_element_t...]
    scatter-add x2 -> x0, local copies, waits for them, and re-layouts: 72.5 us -> none  [the longest x1 36.9 us: shards(): col_init.at[glob_row.reshape(-1), :, local_col.reshape(-1), :]]
    pallas_call x0 -> x5, Pallas kernels: none -> 55.3 us  [the longest x3 47.2 us: tile_call(): pl.pallas_call(functools.partial(tile_kernel, sizes, shifts, segments), o...]
    ppermute x0 -> x31, waiting for transfers between devices: none -> 37.2 us  [the longest x12 29.5 us: flip(): return lambda y: lax.ppermute(y, ('row', 'layer'), pairs)]
    broadcast_in_dim x2 -> x0, local copies, waits for them, and re-layouts: 25.2 us -> none  [the longest x1 12.6 us: shards(): col_init = jnp.zeros((nblk, side, cblk, side), jnp.float32)]
    all_gather x2 -> x0, blocking collectives: 22.1 us -> none  [the longest x1 14.2 us: shards(): lax.all_gather(block_ids.reshape(1, listed), ('row', 'layer'), axis=0, ti...]
    scatter-add x2 -> x0, other arithmetic: 20.6 us -> none  [the longest x1 14.1 us: shards(): col_init.at[glob_row.reshape(-1), :, local_col.reshape(-1), :]]
  transfers between devices with their start and end apart: 4 -> 31, of which waited for: 3 -> 11; matrix products, arithmetic and copies ran while one was open for 7% -> 0% of each run, Pallas kernels for 0% -> 34%
where the time goes in v2:
time: 130 us; the launch traced here: 129 us
  Pallas kernels  55.3 us (43%)
  waiting for transfers between devices  37.2 us (29%)
  starting transfers between devices  20.3 us (16%)
  local copies, waits for them, and re-layouts  13.5 us (10%)
  other arithmetic  1.88 us (1%)
    pallas_call x3, Pallas kernels, tile_call(): pl.pallas_call(functools.partial(tile_kernel, sizes, shifts, segments), o...  47.2 us
    ppermute x12, waiting for transfers between devices, flip(): return lambda y: lax.ppermute(y, ('row', 'layer'), pairs)  29.5 us
    unnamed x52, local copies, waits for them, and re-layouts  13.5 us
    ppermute x12, starting transfers between devices, flip(): return lambda y: lax.ppermute(y, ('row', 'layer'), pairs)  10.1 us
    ppermute x16, starting transfers between devices, sibling(): lax.ppermute(y, 'layer', [(i, n_layer - 1 - i) for i in range(n_layer)])  8.95 us
    pallas_call x2, Pallas kernels, panel_call(): pl.pallas_call(functools.partial(panel_kernel, sizes, kind, segments), ou...  8.09 us
    ppermute x16, waiting for transfers between devices, sibling(): lax.ppermute(y, 'layer', [(i, n_layer - 1 - i) for i in range(n_layer)])  4.26 us
    ppermute x3, waiting for transfers between devices, ring(): return lax.ppermute(y, 'col', [(i, (i + 1) % n_col) for i in range(n_col)])  3.42 us
  transfers between devices with their start and end apart: 31, of which 11 were waited for; matrix products, arithmetic and copies ran while one was open for 0% of the time, Pallas kernels for 34%

profile of v2, /device:TPU:1, one launch (start us, length us, event | category | flops | bytes accessed | tf_op | source)
XLA Modules:
  0.0 129.1 jit_solution(549951549338007023)
XLA Ops:
  1.4 1.1 select_maximum_fusion.refs_0_.refs_9_
  2.6 2.7 %collective-permute-start.2 = (f32[1032,128]{1,0:T(8,128)S(1)}, f32[1032,128]{1,0:T(8,128)S(1)}, u32[]{:S(2)}, u32[]{:S(2)}) collective-permute-start(f32[1032,128]{1,0:T(8,128)S(1)} %select_maximum_fusion.refs_0_.refs_9_), channel_id=1, source_target_pairs={{0,16},{1,9},{8,24},{9,1},{16,0},{17,25},{24,8},{25,17},{2,18},{3,... | collective-permute-start | bytes 1585160 | tf_op jit(solution)/shard_map/ppermute | solution.py:307
  5.2 1.2 collective-permute-start.1
  6.5 1.3 %collective-permute-start = (f32[1032,128]{1,0:T(8,128)S(1)}, f32[1032,128]{1,0:T(8,128)S(1)}, u32[]{:S(2)}, u32[]{:S(2)}) collective-permute-start(f32[1032,128]{1,0:T(8,128)S(1)} %select_maximum_fusion.refs_0_.refs_9_), channel_id=1, source_target_pairs={{0,2},{2,4},{4,6},{6,0},{1,3},{3,5},{5,7},{7,1},{8,10},{10,12},{12... | collective-permute-start | bytes 1585160 | tf_op jit(solution)/shard_map/ppermute | solution.py:312
  7.8 7.6 %collective-permute-done.2.refs_2_.refs_11_ = f32[1032,128]{1,0:T(8,128)S(1)} collective-permute-done((f32[1032,128]{1,0:T(8,128)S(1)}, f32[1032,128]{1,0:T(8,128)S(1)}, u32[]{:S(2)}, u32[]{:S(2)}) %collective-permute-start.2) | collective-permute-done | bytes 528416 | tf_op jit(solution)/shard_map/ppermute | solution.py:307
  15.4 2.7 %collective-permute-done.1.refs_1_.refs_10_ = f32[1032,128]{1,0:T(8,128)S(1)} collective-permute-done((f32[1032,128]{1,0:T(8,128)S(1)}, f32[1032,128]{1,0:T(8,128)S(1)}, u32[]{:S(2)}, u32[]{:S(2)}) %collective-permute-start.1) | collective-permute-done | bytes 528416 | tf_op jit(solution)/shard_map/ppermute | solution.py:307
  18.1 3.2 %collective-permute-done.refs_1_.refs_9_ = f32[1032,128]{1,0:T(8,128)S(1)} collective-permute-done((f32[1032,128]{1,0:T(8,128)S(1)}, f32[1032,128]{1,0:T(8,128)S(1)}, u32[]{:S(2)}, u32[]{:S(2)}) %collective-permute-start) | collective-permute-done | bytes 528416 | tf_op jit(solution)/shard_map/ppermute | solution.py:312
  21.3 1.4 %collective-permute-start.10 = (f32[1032,128]{1,0:T(8,128)S(1)}, f32[1032,128]{1,0:T(8,128)S(1)}, u32[]{:S(2)}, u32[]{:S(2)}) collective-permute-start(f32[1032,128]{1,0:T(8,128)S(1)} %collective-permute-done.2.refs_2_.refs_11_), channel_id=1, source_target_pairs={{0,1},{1,0},{2,3},{3,2},{4,5},{5,4},{6,7},{7,6},{8,9},{9,8},{10,11... | collective-permute-start | bytes 1585160 | tf_op jit(solution)/shard_map/ppermute | solution.py:315
  28.5 4.6 %collective-permute-done.5.refs_3_.refs_12_ = f32[1032,128]{1,0:T(8,128)S(1)} collective-permute-done((f32[1032,128]{1,0:T(8,128)S(1)}, f32[1032,128]{1,0:T(8,128)S(1)}, u32[]{:S(2)}, u32[]{:S(2)}) %collective-permute-start.5) | collective-permute-done | bytes 528416 | tf_op jit(solution)/shard_map/ppermute | solution.py:307
  33.1 10.2 %collective-permute-done.7.refs_11_ = f32[1032,128]{1,0:T(8,128)S(1)} collective-permute-done((f32[1032,128]{1,0:T(8,128)S(1)}, f32[1032,128]{1,0:T(8,128)S(1)}, u32[]{:S(2)}, u32[]{:S(2)}) %collective-permute-start.7) | collective-permute-done | bytes 528416 | tf_op jit(solution)/shard_map/ppermute | solution.py:307
  43.3 1.4 %collective-permute-start.18 = (f32[1032,128]{1,0:T(8,128)S(1)}, f32[1032,128]{1,0:T(8,128)S(1)}, u32[]{:S(2)}, u32[]{:S(2)}) collective-permute-start(f32[1032,128]{1,0:T(8,128)S(1)} %collective-permute-done.7.refs_11_), channel_id=1, source_target_pairs={{0,1},{1,0},{2,3},{3,2},{4,5},{5,4},{6,7},{7,6},{8,9},{9,8},{10,11... | collective-permute-start | bytes 1585160 | tf_op jit(solution)/shard_map/ppermute | solution.py:315
  46.8 1.2 collective-permute-start.12
  50.2 1.2 collective-permute-start.13
  52.3 1.0 copy-done.3
  58.6 3.8 %right_panel.1 = (bf16[64,128,256]{2,1,0:T(8,128)(2,1)S(1)}, s32[48]{0:T(128)S(1)}, s32[64]{0:T(128)S(1)}, s32[64]{0:T(128)S(1)}) custom-call(s32[3]{0:T(128)S(1)} %pad_add_fusion.where_ref.refs_0_, f32[1032,128]{1,0:T(8,128)S(1)} %select_maximum_fusion.refs_0_.refs_9_, f32[1032,128]{1,0:T(8,128)S(1)} %copy-done.6, f32[1032,128]{1,0:T(8,128)S(1)} %copy-done.3, ...), custom_call_target="tpu_custom_call" | custom-call | tf_op jit(solution)/shard_map/right_panel/pallas_call | solution.py:119
  62.4 4.4 %collective-permute-done.14.refs_15_ = f32[1032,128]{1,0:T(8,128)} collective-permute-done((f32[1032,128]{1,0:T(8,128)S(1)}, f32[1032,128]{1,0:T(8,128)}, u32[]{:S(2)}, u32[]{:S(2)}) %collective-permute-start.14) | collective-permute-done | bytes 528416 | tf_op jit(solution)/shard_map/ppermute | solution.py:307
  67.0 1.4 %collective-permute-start.23 = (f32[1032,128]{1,0:T(8,128)}, f32[1032,128]{1,0:T(8,128)S(1)}, u32[]{:S(2)}, u32[]{:S(2)}) collective-permute-start(f32[1032,128]{1,0:T(8,128)} %collective-permute-done.12.refs_12_), channel_id=1, source_target_pairs={{0,1},{1,0},{2,3},{3,2},{4,5},{5,4},{6,7},{7,6},{8,9},{9,8},{10,11... | collective-permute-start | bytes 1585160 | tf_op jit(solution)/shard_map/ppermute | solution.py:315
  69.5 1.4 %collective-permute-done.23.refs_20_ = f32[1032,128]{1,0:T(8,128)S(1)} collective-permute-done((f32[1032,128]{1,0:T(8,128)}, f32[1032,128]{1,0:T(8,128)S(1)}, u32[]{:S(2)}, u32[]{:S(2)}) %collective-permute-start.23) | collective-permute-done | bytes 528416 | tf_op jit(solution)/shard_map/ppermute | solution.py:315
  72.1 4.3 %left_panel.1 = (bf16[64,128,256]{2,1,0:T(8,128)(2,1)S(1)}, s32[48]{0:T(128)S(1)}, s32[64]{0:T(128)S(1)}, s32[64]{0:T(128)S(1)}) custom-call(s32[3]{0:T(128)S(1)} %pad_add_fusion.where_ref.refs_0_, f32[1032,128]{1,0:T(8,128)S(1)} %select_maximum_fusion.refs_0_.refs_9_, f32[1032,128]{1,0:T(8,128)S(1)} %collective-permute-done.refs_1_.refs_9_, ...), custom_call_target="tpu_custom_call" | custom-call | tf_op jit(solution)/shard_map/left_panel/pallas_call | solution.py:119
  76.5 12.8 %tiles_0.1.refs_25_ = f32[768,1536]{1,0:T(8,128)} custom-call(s32[3]{0:T(128)S(1)} %pad_add_fusion.where_ref.refs_0_, s32[48]{0:T(128)S(1)} %get-tuple-element.110.refs_1_, s32[64]{0:T(128)S(1)} %get-tuple-element.111.refs_2_, s32[64]{0:T(128)S(1)} %get-tuple-element.112.refs_3_, s32[48]{0:T(128)S(1)} %get-tuple-element.113.refs_4_, ...), custom_call_target="tpu_custom_call" | custom-call | tf_op jit(solution)/shard_map/tiles_0/pallas_call | solution.py:274
  89.4 1.3 collective-permute-start.27
  92.2 22.9 %tiles_1_2.1.refs_17_ = f32[768,1536]{1,0:T(8,128)} custom-call(s32[3]{0:T(128)S(1)} %pad_add_fusion.where_ref.refs_0_, s32[48]{0:T(128)S(1)} %get-tuple-element.110.refs_1_, s32[64]{0:T(128)S(1)} %get-tuple-element.111.refs_2_, s32[64]{0:T(128)S(1)} %get-tuple-element.112.refs_3_, s32[48]{0:T(128)S(1)} %get-tuple-element.113.refs_4_, ...), custom_call_target="tpu_custom_call" | custom-call | tf_op jit(solution)/shard_map/tiles_1_2/pallas_call | solution.py:274
  116.1 1.5 %collective-permute-done.30.refs_16_ = f32[1032,128]{1,0:T(8,128)S(1)} collective-permute-done((f32[1032,128]{1,0:T(8,128)S(1)}, f32[1032,128]{1,0:T(8,128)S(1)}, u32[]{:S(2)}, u32[]{:S(2)}) %collective-permute-start.30) | collective-permute-done | bytes 528416 | tf_op jit(solution)/shard_map/ppermute | solution.py:315
  117.6 11.5 %tiles_3.1 = f32[768,1536]{1,0:T(8,128)} custom-call(s32[3]{0:T(128)S(1)} %pad_add_fusion.where_ref.refs_0_, s32[48]{0:T(128)S(1)} %get-tuple-element.110.refs_1_, s32[64]{0:T(128)S(1)} %get-tuple-element.111.refs_2_, s32[64]{0:T(128)S(1)} %get-tuple-element.112.refs_3_, s32[48]{0:T(128)S(1)} %get-tuple-element.113.refs_4_, ...), custom_call_target="tpu_custom_call" | custom-call | tf_op jit(solution)/shard_map/tiles_3/pallas_call | solution.py:274
  (98 shorter events, 21.8 us)
Async XLA Ops:
  2.5 5.3 %collective-permute-start.3 = (f32[1032,128]{1,0:T(8,128)S(1)}, f32[1032,128]{1,0:T(8,128)S(1)}, u32[]{:S(2)}, u32[]{:S(2)}) collective-permute-start(f32[1032,128]{1,0:T(8,128)S(1)} %select_maximum_fusion.refs_0_.refs_9_), channel_id=1, source_target_pairs={{0,1},{1,0},{2,3},{3,2},{4,5},{5,4},{6,7},{7,6},{8,9},{9,8},{10,11... | collective-permute-start | bytes 1585160 | tf_op jit(solution)/shard_map/ppermute | solution.py:315
  2.6 12.8 %collective-permute-start.2 = (f32[1032,128]{1,0:T(8,128)S(1)}, f32[1032,128]{1,0:T(8,128)S(1)}, u32[]{:S(2)}, u32[]{:S(2)}) collective-permute-start(f32[1032,128]{1,0:T(8,128)S(1)} %select_maximum_fusion.refs_0_.refs_9_), channel_id=1, source_target_pairs={{0,16},{1,9},{8,24},{9,1},{16,0},{17,25},{24,8},{25,17},{2,18},{3,... | collective-permute-start | bytes 1585160 | tf_op jit(solution)/shard_map/ppermute | solution.py:307
  5.2 12.9 %collective-permute-start.1 = (f32[1032,128]{1,0:T(8,128)S(1)}, f32[1032,128]{1,0:T(8,128)S(1)}, u32[]{:S(2)}, u32[]{:S(2)}) collective-permute-start(f32[1032,128]{1,0:T(8,128)S(1)} %select_maximum_fusion.refs_0_.refs_9_), channel_id=1, source_target_pairs={{0,8},{1,17},{8,0},{9,25},{16,24},{17,1},{24,16},{25,9},{2,10},{3,... | collective-permute-start | bytes 1585160 | tf_op jit(solution)/shard_map/ppermute | solution.py:307
  6.5 14.8 %collective-permute-start = (f32[1032,128]{1,0:T(8,128)S(1)}, f32[1032,128]{1,0:T(8,128)S(1)}, u32[]{:S(2)}, u32[]{:S(2)}) collective-permute-start(f32[1032,128]{1,0:T(8,128)S(1)} %select_maximum_fusion.refs_0_.refs_9_), channel_id=1, source_target_pairs={{0,2},{2,4},{4,6},{6,0},{1,3},{3,5},{5,7},{7,1},{8,10},{10,12},{12... | collective-permute-start | bytes 1585160 | tf_op jit(solution)/shard_map/ppermute | solution.py:312
  23.6 9.5 %collective-permute-start.5 = (f32[1032,128]{1,0:T(8,128)S(1)}, f32[1032,128]{1,0:T(8,128)S(1)}, u32[]{:S(2)}, u32[]{:S(2)}) collective-permute-start(f32[1032,128]{1,0:T(8,128)S(1)} %collective-permute-done.1.refs_1_.refs_10_), channel_id=1, source_target_pairs={{0,16},{1,9},{8,24},{9,1},{16,0},{17,25},{24,8},{25,17},{2,18},{3,... | collective-permute-start | bytes 1585160 | tf_op jit(solution)/shard_map/ppermute | solution.py:307
  24.6 8.4 %collective-permute-start.8 = (f32[1032,128]{1,0:T(8,128)S(1)}, f32[1032,128]{1,0:T(8,128)S(1)}, u32[]{:S(2)}, u32[]{:S(2)}) collective-permute-start(f32[1032,128]{1,0:T(8,128)S(1)} %collective-permute-done.refs_1_.refs_9_), channel_id=1, source_target_pairs={{0,1},{1,0},{2,3},{3,2},{4,5},{5,4},{6,7},{7,6},{8,9},{9,8},{10,11... | collective-permute-start | bytes 1585160 | tf_op jit(solution)/shard_map/ppermute | solution.py:315
  25.4 17.9 %collective-permute-start.7 = (f32[1032,128]{1,0:T(8,128)S(1)}, f32[1032,128]{1,0:T(8,128)S(1)}, u32[]{:S(2)}, u32[]{:S(2)}) collective-permute-start(f32[1032,128]{1,0:T(8,128)S(1)} %collective-permute-done.refs_1_.refs_9_), channel_id=1, source_target_pairs={{0,16},{1,9},{8,24},{9,1},{16,0},{17,25},{24,8},{25,17},{2,18},{3,... | collective-permute-start | bytes 1585160 | tf_op jit(solution)/shard_map/ppermute | solution.py:307
  26.6 16.6 %collective-permute-start.6 = (f32[1032,128]{1,0:T(8,128)S(1)}, f32[1032,128]{1,0:T(8,128)}, u32[]{:S(2)}, u32[]{:S(2)}) collective-permute-start(f32[1032,128]{1,0:T(8,128)S(1)} %collective-permute-done.refs_1_.refs_9_), channel_id=1, source_target_pairs={{0,8},{1,17},{8,0},{9,25},{16,24},{17,1},{24,16},{25,9},{2,10},{3,... | collective-permute-start | bytes 1585160 | tf_op jit(solution)/shard_map/ppermute | solution.py:307
  28.5 14.8 %collective-permute-start.4 = (f32[1032,128]{1,0:T(8,128)S(1)}, f32[1032,128]{1,0:T(8,128)S(1)}, u32[]{:S(2)}, u32[]{:S(2)}) collective-permute-start(f32[1032,128]{1,0:T(8,128)S(1)} %collective-permute-done.refs_1_.refs_9_), channel_id=1, source_target_pairs={{0,2},{2,4},{4,6},{6,0},{1,3},{3,5},{5,7},{7,1},{8,10},{10,12},{12... | collective-permute-start | bytes 1585160 | tf_op jit(solution)/shard_map/ppermute | solution.py:312
  43.3 4.7 %collective-permute-start.18 = (f32[1032,128]{1,0:T(8,128)S(1)}, f32[1032,128]{1,0:T(8,128)S(1)}, u32[]{:S(2)}, u32[]{:S(2)}) collective-permute-start(f32[1032,128]{1,0:T(8,128)S(1)} %collective-permute-done.7.refs_11_), channel_id=1, source_target_pairs={{0,1},{1,0},{2,3},{3,2},{4,5},{5,4},{6,7},{7,6},{8,9},{9,8},{10,11... | collective-permute-start | bytes 1585160 | tf_op jit(solution)/shard_map/ppermute | solution.py:315
  45.5 5.9 %collective-permute-start.16 = (f32[1032,128]{1,0:T(8,128)S(1)}, f32[1032,128]{1,0:T(8,128)S(1)}, u32[]{:S(2)}, u32[]{:S(2)}) collective-permute-start(f32[1032,128]{1,0:T(8,128)S(1)} %collective-permute-done.5.refs_3_.refs_12_), channel_id=1, source_target_pairs={{0,1},{1,0},{2,3},{3,2},{4,5},{5,4},{6,7},{7,6},{8,9},{9,8},{10,11... | collective-permute-start | bytes 1585160 | tf_op jit(solution)/shard_map/ppermute | solution.py:315
  46.8 15.6 %collective-permute-start.12 = (f32[1032,128]{1,0:T(8,128)}, f32[1032,128]{1,0:T(8,128)}, u32[]{:S(2)}, u32[]{:S(2)}) collective-permute-start(f32[1032,128]{1,0:T(8,128)} %collective-permute-done.6.refs_10_), channel_id=1, source_target_pairs={{0,16},{1,9},{8,24},{9,1},{16,0},{17,25},{24,8},{25,17},{2,18},{3,... | collective-permute-start | bytes 1585160 | tf_op jit(solution)/shard_map/ppermute | solution.py:307
  48.0 14.4 %collective-permute-start.15 = (f32[1032,128]{1,0:T(8,128)S(1)}, f32[1032,128]{1,0:T(8,128)}, u32[]{:S(2)}, u32[]{:S(2)}) collective-permute-start(f32[1032,128]{1,0:T(8,128)S(1)} %collective-permute-done.4.refs_2_.refs_13_), channel_id=1, source_target_pairs={{0,1},{1,0},{2,3},{3,2},{4,5},{5,4},{6,7},{7,6},{8,9},{9,8},{10,11... | collective-permute-start | bytes 1585160 | tf_op jit(solution)/shard_map/ppermute | solution.py:315
  48.9 18.0 %collective-permute-start.14 = (f32[1032,128]{1,0:T(8,128)S(1)}, f32[1032,128]{1,0:T(8,128)}, u32[]{:S(2)}, u32[]{:S(2)}) collective-permute-start(f32[1032,128]{1,0:T(8,128)S(1)} %collective-permute-done.4.refs_2_.refs_13_), channel_id=1, source_target_pairs={{0,16},{1,9},{8,24},{9,1},{16,0},{17,25},{24,8},{25,17},{2,18},{3,... | collective-permute-start | bytes 1585160 | tf_op jit(solution)/shard_map/ppermute | solution.py:307
  50.2 16.7 %collective-permute-start.13 = (f32[1032,128]{1,0:T(8,128)S(1)}, f32[1032,128]{1,0:T(8,128)}, u32[]{:S(2)}, u32[]{:S(2)}) collective-permute-start(f32[1032,128]{1,0:T(8,128)S(1)} %collective-permute-done.4.refs_2_.refs_13_), channel_id=1, source_target_pairs={{0,8},{1,17},{8,0},{9,25},{16,24},{17,1},{24,16},{25,9},{2,10},{3,... | collective-permute-start | bytes 1585160 | tf_op jit(solution)/shard_map/ppermute | solution.py:307
  52.2 14.8 %collective-permute-start.11 = (f32[1032,128]{1,0:T(8,128)S(1)}, f32[1032,128]{1,0:T(8,128)S(1)}, u32[]{:S(2)}, u32[]{:S(2)}) collective-permute-start(f32[1032,128]{1,0:T(8,128)S(1)} %collective-permute-done.4.refs_2_.refs_13_), channel_id=1, source_target_pairs={{0,2},{2,4},{4,6},{6,0},{1,3},{3,5},{5,7},{7,1},{8,10},{10,12},{12... | collective-permute-start | bytes 1585160 | tf_op jit(solution)/shard_map/ppermute | solution.py:312
  68.4 20.9 %collective-permute-start.24 = (f32[1032,128]{1,0:T(8,128)}, f32[1032,128]{1,0:T(8,128)S(1)}, u32[]{:S(2)}, u32[]{:S(2)}) collective-permute-start(f32[1032,128]{1,0:T(8,128)} %collective-permute-done.13.refs_14_), channel_id=1, source_target_pairs={{0,1},{1,0},{2,3},{3,2},{4,5},{5,4},{6,7},{7,6},{8,9},{9,8},{10,11... | collective-permute-start | bytes 1585160 | tf_op jit(solution)/shard_map/ppermute | solution.py:315
  68.9 20.4 %collective-permute-start.19 = (f32[1032,128]{1,0:T(8,128)}, f32[1032,128]{1,0:T(8,128)S(1)}, u32[]{:S(2)}, u32[]{:S(2)}) collective-permute-start(f32[1032,128]{1,0:T(8,128)} %collective-permute-done.13.refs_14_), channel_id=1, source_target_pairs={{0,16},{1,9},{8,24},{9,1},{16,0},{17,25},{24,8},{25,17},{2,18},{3,... | collective-permute-start | bytes 1585160 | tf_op jit(solution)/shard_map/ppermute | solution.py:307
  69.4 19.9 %collective-permute-start.25 = (f32[1032,128]{1,0:T(8,128)}, f32[1032,128]{1,0:T(8,128)S(1)}, u32[]{:S(2)}, u32[]{:S(2)}) collective-permute-start(f32[1032,128]{1,0:T(8,128)} %collective-permute-done.14.refs_15_), channel_id=1, source_target_pairs={{0,1},{1,0},{2,3},{3,2},{4,5},{5,4},{6,7},{7,6},{8,9},{9,8},{10,11... | collective-permute-start | bytes 1585160 | tf_op jit(solution)/shard_map/ppermute | solution.py:315
  70.9 18.5 %collective-permute-start.21 = (f32[1032,128]{1,0:T(8,128)S(1)}, f32[1032,128]{1,0:T(8,128)S(1)}, u32[]{:S(2)}, u32[]{:S(2)}) collective-permute-start(f32[1032,128]{1,0:T(8,128)S(1)} %collective-permute-done.11.refs_3_.refs_9_), channel_id=1, source_target_pairs={{0,16},{1,9},{8,24},{9,1},{16,0},{17,25},{24,8},{25,17},{2,18},{3,... | collective-permute-start | bytes 1585160 | tf_op jit(solution)/shard_map/ppermute | solution.py:307
  71.4 18.0 %collective-permute-start.20 = (f32[1032,128]{1,0:T(8,128)S(1)}, f32[1032,128]{1,0:T(8,128)S(1)}, u32[]{:S(2)}, u32[]{:S(2)}) collective-permute-start(f32[1032,128]{1,0:T(8,128)S(1)} %collective-permute-done.11.refs_3_.refs_9_), channel_id=1, source_target_pairs={{0,8},{1,17},{8,0},{9,25},{16,24},{17,1},{24,16},{25,9},{2,10},{3,... | collective-permute-start | bytes 1585160 | tf_op jit(solution)/shard_map/ppermute | solution.py:307
  90.7 24.4 %collective-permute-start.29 = (f32[1032,128]{1,0:T(8,128)S(1)}, f32[1032,128]{1,0:T(8,128)S(1)}, u32[]{:S(2)}, u32[]{:S(2)}) collective-permute-start(f32[1032,128]{1,0:T(8,128)S(1)} %collective-permute-done.21.refs_11_), channel_id=1, source_target_pairs={{0,1},{1,0},{2,3},{3,2},{4,5},{5,4},{6,7},{7,6},{8,9},{9,8},{10,11... | collective-permute-start | bytes 1585160 | tf_op jit(solution)/shard_map/ppermute | solution.py:315
  90.7 24.4 %collective-permute-start.28 = (f32[1032,128]{1,0:T(8,128)S(1)}, f32[1032,128]{1,0:T(8,128)S(1)}, u32[]{:S(2)}, u32[]{:S(2)}) collective-permute-start(f32[1032,128]{1,0:T(8,128)S(1)} %collective-permute-done.20.refs_10_), channel_id=1, source_target_pairs={{0,1},{1,0},{2,3},{3,2},{4,5},{5,4},{6,7},{7,6},{8,9},{9,8},{10,11... | collective-permute-start | bytes 1585160 | tf_op jit(solution)/shard_map/ppermute | solution.py:315
  91.2 23.9 %collective-permute-start.26 = (f32[1032,128]{1,0:T(8,128)S(1)}, f32[1032,128]{1,0:T(8,128)S(1)}, u32[]{:S(2)}, u32[]{:S(2)}) collective-permute-start(f32[1032,128]{1,0:T(8,128)S(1)} %collective-permute-done.20.refs_10_), channel_id=1, source_target_pairs={{0,16},{1,9},{8,24},{9,1},{16,0},{17,25},{24,8},{25,17},{2,18},{3,... | collective-permute-start | bytes 1585160 | tf_op jit(solution)/shard_map/ppermute | solution.py:307
  (33 other events, 247.7 us)

commit v3 on v2

v3 whole, which is shorter than its diff:
```python
import functools

import jax
import jax.numpy as jnp
from jax import lax
from jax.experimental import pallas as pl
from jax.experimental.pallas import tpu as pltpu
from jax.sharding import PartitionSpec as P

ROW_BLOCKS = 12
GROUP = 4
AHEAD = (0, 1, 2, 3)
LATER = (0, 1, 1, 1)
CUBES = 8
CHUNK = 128
STRIP = 384
PANEL_MB = 61
TILE_MB = 61
AXES = ("row", "col", "layer")
VMEM = pl.BlockSpec(memory_space=pltpu.VMEM)
SMEM = pl.BlockSpec(memory_space=pltpu.SMEM)
HBM = pl.BlockSpec(memory_space=pltpu.HBM)


def params(megabytes):
    return pltpu.CompilerParams(vmem_limit_bytes=megabytes * 1024 * 1024)


def split(x):
    high = x.astype(jnp.bfloat16)
    low = (x - high.astype(jnp.float32)).astype(jnp.bfloat16)
    return high, low


def product(left, right):
    part = jnp.dot(
        left, jnp.concatenate([right, right], axis=0), preferred_element_type=jnp.float32
    )
    side = right.shape[0]
    return part[:, :side] + part[:, side:]


def lanes(i, side):
    return pl.ds(pl.multiple_of(i * side, side), side)


def start_copies(side, listed, array_refs, buffer, lists, sem):
    out = []
    for i, ref in enumerate(array_refs):
        value = pltpu.make_async_copy(
            ref.at[pl.ds(0, listed * side)],
            buffer.at[pl.ds(i * listed * side, listed * side)],
            sem.at[0, i],
        )
        names = pltpu.make_async_copy(
            ref.at[pl.ds(listed * side, 1)], lists.at[pl.ds(i, 1)], sem.at[1, i]
        )
        value.start()
        names.start()
        out.append((value, names))
    return out


def tile_row(segment, my_row, my_layer, n_layer):
    first, second, _, other = segment
    layer = (n_layer - 1 - my_layer) if other else my_layer
    return my_row ^ jnp.where(layer == 0, first, second)


def panel_kernel(sizes, segments, where_ref, *refs):
    n_row, n_col, n_layer, listed, side = sizes
    arrays = len(segments)
    array_refs = refs[:arrays]
    panel, table, buffer, lists, sem = refs[arrays:]
    nblk = ROW_BLOCKS * n_row
    cblk = nblk // n_col
    half = ROW_BLOCKS // n_layer
    my_col, my_layer = where_ref[1], where_ref[2]
    moves = start_copies(side, listed, array_refs, buffer, lists, sem)
    nxt, tag = nblk, nblk + arrays * listed
    total = tag + arrays * listed

    def clear(i, _):
        table[i] = -1
        return 0

    lax.fori_loop(0, nblk, clear, 0)
    count = jnp.int32(0)
    for i, (value, names) in enumerate(moves):
        names.wait()
        value.wait()
        first = lax.rem(my_col + (n_col - segments[i][2]), n_col) * cblk

        def one(s, count, i=i, first=first):
            code = lists[i, s].astype(jnp.int32)
            key = first + (code & 15)
            mark = (code >> 4) - my_layer * half
            use = (code >= 0) & (mark >= 0) & (mark < half)

            @pl.when(use)
            def _():
                table[nxt + count] = table[key]
                table[key] = count
                table[tag + count] = mark
                high, low = split(buffer[lanes(i * listed + s, side), :])
                panel[count, :, :side] = high
                panel[count, :, side:] = low

            return count + use.astype(jnp.int32)

        count = lax.fori_loop(0, listed, one, count)
    table[total] = count
    for i in range(3):
        table[total + 1 + i] = where_ref[i]


def panel_call(sizes, segments, arrays, where):
    n_row, n_col, n_layer, listed, side = sizes
    nblk = ROW_BLOCKS * n_row
    total = len(segments) * listed
    return pl.pallas_call(
        functools.partial(panel_kernel, sizes, segments),
        out_shape=[
            jax.ShapeDtypeStruct((total, side, 2 * side), jnp.bfloat16),
            jax.ShapeDtypeStruct((nblk + 2 * total + 4,), jnp.int32),
        ],
        in_specs=[SMEM] + [HBM] * len(arrays),
        out_specs=[VMEM, SMEM],
        scratch_shapes=[
            pltpu.VMEM((total * side, side), jnp.float32),
            pltpu.SMEM((len(segments), side), jnp.float32),
            pltpu.SemaphoreType.DMA((2, len(segments))),
        ],
        compiler_params=params(max(PANEL_MB, total // 4)),
        name="left_panel",
    )(where, *arrays)


def tile_kernel(sizes, shifts, segments, *refs):
    n_row, n_col, n_layer, listed, side = sizes
    arrays = len(segments)
    table, left_ref = refs[:2]
    array_refs = refs[2 : 2 + arrays]
    rest = refs[2 + arrays :]
    if shifts[0]:
        column_refs, before, rest = rest[: n_layer * 4], rest[n_layer * 4], rest[n_layer * 4 + 1 :]
    else:
        column_refs = array_refs
    (out_hbm, buffer, lists, sem, left, left_sem, column, column_lists, column_sem) = rest[:9]
    late, out_sem, out_ref, right, panel, square, wide, plan, cubes = rest[9:]
    nblk = ROW_BLOCKS * n_row
    cblk = nblk // n_col
    rows = ROW_BLOCKS // n_layer * side
    pairs = n_layer * listed
    nxt, tag = nblk, nblk + left.shape[0]
    total = tag + left.shape[0]
    my_row, my_col, my_layer = table[total + 1], table[total + 2], table[total + 3]
    moves = start_copies(side, listed, array_refs, buffer, lists, sem)

    def get_left(i):
        part = pl.ds(pl.multiple_of(i * listed, listed), listed)
        return pltpu.make_async_copy(left_ref.at[part], left.at[part], left_sem.at[i])

    def each_left(step):
        def one(i, _):
            step(get_left(i))
            return 0

        lax.fori_loop(0, (table[total] + listed - 1) // listed, one, 0)

    each_left(lambda copy: copy.start())

    cols = [lax.rem(my_col + (n_col - shift), n_col) for shift in shifts]
    meets = [col * cblk // ROW_BLOCKS for col in cols]

    def get_column(t, ref, copy):
        at = (t * n_layer + copy) * listed * side
        return (
            pltpu.make_async_copy(
                ref.at[pl.ds(0, listed * side)],
                column.at[pl.ds(at, listed * side)],
                column_sem.at[0, t * n_layer + copy],
            ),
            pltpu.make_async_copy(
                ref.at[pl.ds(listed * side, 1)],
                column_lists.at[pl.ds(t * n_layer + copy, 1)],
                column_sem.at[1, t * n_layer + copy],
            ),
        )

    for t in range(len(shifts)):
        for i in range(n_layer * 4):
            first, second, _, other = segments[i % 4]
            copy = i // 4
            layer = (n_layer - 1 - my_layer) if copy else my_layer

            @pl.when((my_row ^ jnp.where(layer == 0, first, second)) == meets[t])
            def _(t=t, i=i, copy=copy):
                for move in get_column(t, column_refs[i], copy):
                    move.start()

    def put(i):
        line = pl.ds(pl.multiple_of(i * STRIP, STRIP), STRIP)
        return pltpu.make_async_copy(out_ref.at[line], out_hbm.at[line], out_sem.at[i])

    if shifts[0]:
        get_before = pltpu.make_async_copy(before, out_ref, late)
        get_before.start()

    for t, shift in enumerate(shifts):

        def zero(j, _):
            square[j] = jnp.zeros((rows, side), jnp.float32)
            return 0

        lax.fori_loop(0, cblk, zero, 0)
        count = jnp.int32(0)
        for i, (value, names) in enumerate(moves):
            if segments[i][2] != shift:
                continue
            names.wait()
            value.wait()
            row0 = tile_row(segments[i], my_row, my_layer, n_layer) * ROW_BLOCKS

            def one(s, count, i=i, row0=row0):
                code = lists[i, s].astype(jnp.int32)
                local = code & 15
                first = jnp.where(code >= 0, table[jnp.maximum(row0 + (code >> 4), 0)], -1)
                at = i * listed + s

                @pl.when(first >= 0)
                def _():
                    high, low = split(buffer[lanes(at, side), :])
                    right[at, :, :side] = high
                    right[at, :, side:] = low

                def more(carry):
                    return carry[0] >= 0

                def add(carry):
                    a, count = carry
                    plan[0, count] = a
                    plan[1, count] = at
                    plan[2, count] = local
                    plan[3, count] = table[tag + a]
                    return table[nxt + a], count + 1

                return lax.while_loop(more, add, (first, count))[1]

            count = lax.fori_loop(0, listed, one, count)

        for u in range(GROUP - 1):
            plan[0, count + u] = 0
            plan[1, count + u] = 0
            plan[2, count + u] = cblk
            plan[3, count + u] = 0

        def group(g, _):
            parts = []
            for u in range(GROUP):
                e = g * GROUP + u
                parts.append(product(left[plan[0, e]], right[plan[1, e]]))
            for u in range(GROUP):
                e = g * GROUP + u
                at = lanes(plan[3, e], side)
                j = plan[2, e]
                square[j, at, :] = square[j, at, :] + parts[u]
            return 0

        if not t:
            each_left(lambda copy: copy.wait())
        lax.fori_loop(0, (count + GROUP - 1) // GROUP, group, 0)
        if not shift:

            def begin(j, _):
                out_ref[:, lanes(j, side)] = 3.0 * square[j]
                return 0

            lax.fori_loop(0, cblk, begin, 0)
        elif not t:
            get_before.wait()

        def widen(j, _):
            high, low = split(-2.0 * square[j])
            wide[j, :, :side] = high
            wide[j, :, side:] = low
            return 0

        lax.fori_loop(0, cblk, widen, 0)
        for copy in range(n_layer):
            for move in get_column(t, column_refs[0], copy):
                move.wait()
        start = meets[t] * ROW_BLOCKS - cols[t] * cblk

        def note(e, count, t=t, start=start):
            copy = e // listed
            code = column_lists[t * n_layer + copy, e - copy * listed].astype(jnp.int32)
            j = start + (code >> 4)
            use = (code >= 0) & (j >= 0) & (j < cblk)

            @pl.when(use)
            def _():
                high, low = split(column[lanes(t * pairs + e, side), :])
                panel[e, :, :side] = high
                panel[e, :, side:] = low
                cubes[0, count] = e
                cubes[1, count] = j
                cubes[2, count] = code & 15

            return count + use.astype(jnp.int32)

        count = lax.fori_loop(0, pairs, note, jnp.int32(0))
        wide[cblk] = jnp.zeros((rows, 2 * side), jnp.bfloat16)
        for u in range(CUBES - 1):
            cubes[0, count + u] = cubes[0, 0]
            cubes[1, count + u] = cblk
            cubes[2, count + u] = 0

        final = t == len(shifts) - 1

        def strip(i, _, count=count, final=final):
            def cube(g, _):
                for m in range(0, STRIP, CHUNK):
                    line = pl.ds(pl.multiple_of(i * STRIP + m, CHUNK), CHUNK)
                    parts = []
                    for u in range(CUBES):
                        e = g * CUBES + u
                        parts.append(product(wide[cubes[1, e], line, :], panel[cubes[0, e]]))
                    for u in range(CUBES):
                        at = lanes(cubes[2, g * CUBES + u], side)
                        out_ref[line, at] = out_ref[line, at] + parts[u]
                return 0

            lax.fori_loop(0, (count + CUBES - 1) // CUBES, cube, 0)
            if final:
                put(i).start()
            return 0

        lax.fori_loop(0, rows // STRIP, strip, 0)

    def written(i, _):
        put(i).wait()
        return 0

    lax.fori_loop(0, rows // STRIP, written, 0)


def tile_call(sizes, shifts, segments, arrays, lefts, column, before):
    n_row, n_col, n_layer, listed, side = sizes
    nblk = ROW_BLOCKS * n_row
    cblk = nblk // n_col
    half = ROW_BLOCKS // n_layer
    rows = half * side
    total = len(segments) * listed
    pairs = n_layer * listed
    left, table = lefts
    extra = [] if before is None else [*column, before]
    return pl.pallas_call(
        functools.partial(tile_kernel, sizes, shifts, segments),
        out_shape=jax.ShapeDtypeStruct((rows, cblk * side), jnp.float32),
        in_specs=[SMEM] + [HBM] * (1 + len(arrays) + len(extra)),
        out_specs=HBM,
        scratch_shapes=[
            pltpu.VMEM((total * side, side), jnp.float32),
            pltpu.SMEM((len(segments), side), jnp.float32),
            pltpu.SemaphoreType.DMA((2, len(segments))),
            pltpu.VMEM(left.shape, left.dtype),
            pltpu.SemaphoreType.DMA((left.shape[0] // listed,)),
            pltpu.VMEM((len(shifts) * pairs * side, side), jnp.float32),
            pltpu.SMEM((len(shifts) * n_layer, side), jnp.float32),
            pltpu.SemaphoreType.DMA((2, len(shifts) * n_layer)),
            pltpu.SemaphoreType.DMA,
            pltpu.SemaphoreType.DMA((rows // STRIP,)),
            pltpu.VMEM((rows, cblk * side), jnp.float32),
            pltpu.VMEM((total, side, 2 * side), jnp.bfloat16),
            pltpu.VMEM((pairs, side, 2 * side), jnp.bfloat16),
            pltpu.VMEM((cblk + 1, rows, side), jnp.float32),
            pltpu.VMEM((cblk + 1, rows, 2 * side), jnp.bfloat16),
            pltpu.SMEM((4, total * half + GROUP), jnp.int32),
            pltpu.SMEM((3, pairs + CUBES), jnp.int32),
        ],
        compiler_params=params(TILE_MB),
        name="tiles_" + "_".join(str(s) for s in shifts),
    )(table, left, *arrays, *extra)


def shards(blocks, block_ids, counts):
    n_row, n_col, n_layer = (lax.axis_size(a) for a in AXES)
    listed, side = blocks.shape[3], blocks.shape[-1]
    sizes = (n_row, n_col, n_layer, listed, side)
    half = ROW_BLOCKS // n_layer

    def flip(bits, cross=False):
        pairs = []
        for r in range(n_row):
            for k in range(n_layer):
                to = n_layer - 1 - k if cross else k
                pairs.append((r * n_layer + k, (r ^ bits[min(k, 1)]) * n_layer + to))
        return lambda y: lax.ppermute(y, ("row", "layer"), pairs)

    across, along, beside = flip((1, 2)), flip((2, 1)), flip((2, 1), True)

    def ring(y):
        return lax.ppermute(y, "col", [(i, (i + 1) % n_col) for i in range(n_col)])

    def sibling(y):
        return lax.ppermute(y, "layer", [(i, n_layer - 1 - i) for i in range(n_layer)])

    where = jnp.stack([lax.axis_index(a) for a in AXES]).astype(jnp.int32)
    cblk = ROW_BLOCKS * n_row // n_col
    ids = block_ids.reshape(1, listed)
    live = lax.broadcasted_iota(jnp.int32, (1, listed), 1) < counts.reshape(1, 1)
    names = jnp.where(live, ids // cblk * 16 + ids % cblk, -1).astype(jnp.float32)
    names = jnp.pad(names, ((0, 7), (0, side - listed)))
    own = jnp.concatenate([blocks.reshape(listed * side, side), names], axis=0)

    ways = {"A": (0, 0), "U": (1, 2), "V": (2, 1), "D": (3, 3)}
    held = {("A", 0): own}
    twin = {}
    lefts = total = None
    fresh = [("A", 0)]

    def gathered(names):
        segments = [(*ways[k], s, other) for other in (False, True) for k, s in names]
        return segments, [source[name] for source in (held, twin) for name in names]

    def quads(shifts):
        return [(k, s) for s in shifts for k in ways]

    def tiles(shifts, total):
        for i in range(0, len(shifts), 2):
            segments, arrays = gathered(quads(shifts[i : i + 2]))
            column = gathered(quads([0]))[1]
            total = tile_call(
                sizes, tuple(shifts[i : i + 2]), segments, arrays, lefts, column, total
            )
        return total

    rounds = [[] for _ in range(2 * n_col)]
    for s in range(n_col):
        if s:
            rounds[s - 1].append((("A", s), s - 1))
        first = AHEAD[min(s, 3)] + max(0, s - 3)
        there = first + LATER[min(s, 3)]
        rounds[first] += [(("U", s), there), (("V", s), there)]
        rounds[there + 1].append((("D", s), there + 1))
    last = max(t for t in range(2 * n_col) if rounds[t])
    makers = {
        "A": lambda s: ring(held[("A", s - 1)]),
        "U": lambda s: across(held[("A", s)]),
        "V": lambda s: along(held[("A", s)]),
        "D": lambda s: along(held[("U", s)]),
    }
    done = 0
    flying = {}
    for t in range(last + 2):
        for name, there in rounds[t]:
            flying[name] = (makers[name[0]](name[1]), there)
            if t == last:
                twin[name] = beside(held[("U", name[1])])
        twin.update({name: sibling(held[name]) for name in fresh if name not in twin})
        if lefts is None and ("A", n_col - 1) in twin:
            segments, arrays = gathered([("A", s) for s in range(n_col)])
            lefts = panel_call(sizes, segments, arrays, where)
        ready = done
        while lefts is not None and ready < n_col and {("D", ready)} <= held.keys() & twin.keys():
            ready += 1
        total = tiles(list(range(done, ready)), total)
        done = ready
        if t > last:
            return total
        sent = {n: flying.pop(n)[0] for n in list(flying) if flying[n][1] == t}
        copied = {n: twin[n] for n in [*fresh, *sent] if n in twin}
        sent, copied, lefts, total = lax.optimization_barrier((sent, copied, lefts, total))
        held.update(sent)
        twin.update(copied)
        fresh = list(sent)


def solution(mesh):
    return jax.shard_map(
        shards,
        mesh=mesh,
        in_specs=(
            P("row", "col", "layer", None, None, None),
            P("row", "col", "layer", None),
            P("row", "col", "layer"),
        ),
        out_specs=P(("row", "layer"), "col"),
        check_vma=False,
    )
```

time: 130 us -> 127 us (0.977); the launches traced: 129 us -> 124 us
  local copies, waits for them, and re-layouts: 13.5 us -> 2.43 us
  waiting for transfers between devices: 37.2 us -> 43.7 us
  Pallas kernels: 55.3 us -> 50.7 us
  starting transfers between devices: 20.3 us -> 24.3 us
    ppermute x3, waiting for transfers between devices: 3.42 us -> 28 us  [ring(): return lax.ppermute(y, 'col', [(i, (i + 1) % n_col) for i in range(n_col)])]
    ppermute x12 -> x13, waiting for transfers between devices: 29.5 us -> 15.6 us  [flip(): return lambda y: lax.ppermute(y, ('row', 'layer'), pairs)]
    unnamed x52 -> x38, local copies, waits for them, and re-layouts: 13.5 us -> 2.43 us
    ppermute x16 -> x15, waiting for transfers between devices: 4.26 us -> 0.04 us  [sibling(): lax.ppermute(y, 'layer', [(i, n_layer - 1 - i) for i in range(n_layer)])]
    ppermute x12 -> x13, starting transfers between devices: 10.1 us -> 13.4 us  [flip(): return lambda y: lax.ppermute(y, ('row', 'layer'), pairs)]
    pallas_call x2 -> x1, Pallas kernels: 8.09 us -> 5.58 us  [panel_call(): pl.pallas_call(functools.partial(panel_kernel, sizes, segments), out_shap...]
    ppermute x3, starting transfers between devices: 1.3 us -> 3.53 us  [ring(): return lax.ppermute(y, 'col', [(i, (i + 1) % n_col) for i in range(n_col)])]
    pallas_call x3 -> x4, Pallas kernels: 47.2 us -> 45.1 us  [tile_call(): pl.pallas_call(functools.partial(tile_kernel, sizes, shifts, segments), o...]
  transfers between devices with their start and end apart: 31 -> 31, of which waited for: 11 -> 8; matrix products, arithmetic and copies ran while one was open for 0% -> 0% of each run, Pallas kernels for 34% -> 33%
where the time goes in v3:
time: 127 us; the launch traced here: 124 us
  Pallas kernels  50.7 us (40%)
  waiting for transfers between devices  43.7 us (34%)
  starting transfers between devices  24.3 us (19%)
  local copies, waits for them, and re-layouts  2.43 us (2%)
  other arithmetic  2.36 us (2%)
    pallas_call x4, Pallas kernels, tile_call(): pl.pallas_call(functools.partial(tile_kernel, sizes, shifts, segments), o...  45.1 us
    ppermute x3, waiting for transfers between devices, ring(): return lax.ppermute(y, 'col', [(i, (i + 1) % n_col) for i in range(n_col)])  28 us
    ppermute x13, waiting for transfers between devices, flip(): return lambda y: lax.ppermute(y, ('row', 'layer'), pairs)  15.6 us
    ppermute x13, starting transfers between devices, flip(): return lambda y: lax.ppermute(y, ('row', 'layer'), pairs)  13.4 us
    ppermute x15, starting transfers between devices, sibling(): lax.ppermute(y, 'layer', [(i, n_layer - 1 - i) for i in range(n_layer)])  7.35 us
    pallas_call x1, Pallas kernels, panel_call(): pl.pallas_call(functools.partial(panel_kernel, sizes, segments), out_shap...  5.58 us
    ppermute x3, starting transfers between devices, ring(): return lax.ppermute(y, 'col', [(i, (i + 1) % n_col) for i in range(n_col)])  3.53 us
  transfers between devices with their start and end apart: 31, of which 8 were waited for; matrix products, arithmetic and copies ran while one was open for 0% of the time, Pallas kernels for 33%

profile of v3, /device:TPU:1, one launch (start us, length us, event | category | flops | bytes accessed | tf_op | source)
XLA Modules:
  0.0 124.4 jit_solution(17269607264471452159)
XLA Ops:
  2.4 2.2 %collective-permute-start = (f32[1032,128]{1,0:T(8,128)S(1)}, f32[1032,128]{1,0:T(8,128)S(1)}, u32[]{:S(2)}, u32[]{:S(2)}) collective-permute-start(f32[1032,128]{1,0:T(8,128)S(1)} %select_maximum_fusion.refs_0_.refs_2_.refs_10_), channel_id=1, source_target_pairs={{0,2},{2,4},{4,6},{6,0},{1,3},{3,5},{5,7},{7,1},{8,10},{10,12},{12... | collective-permute-start | bytes 1585160 | tf_op jit(solution)/shard_map/ppermute | solution.py:404
  4.6 1.2 collective-permute-start.1
  5.8 1.2 collective-permute-start.2
  7.0 1.5 %collective-permute-start.3 = (f32[1032,128]{1,0:T(8,128)S(1)}, f32[1032,128]{1,0:T(8,128)S(1)}, u32[]{:S(2)}, u32[]{:S(2)}) collective-permute-start(f32[1032,128]{1,0:T(8,128)S(1)} %select_maximum_fusion.refs_0_.refs_2_.refs_10_), channel_id=1, source_target_pairs={{0,1},{1,0},{2,3},{3,2},{4,5},{5,4},{6,7},{7,6},{8,9},{9,8},{10,11... | collective-permute-start | bytes 1585160 | tf_op jit(solution)/shard_map/ppermute | solution.py:407
  8.6 9.8 %collective-permute-done.refs_1_.refs_2_ = f32[1032,128]{1,0:T(8,128)S(1)} collective-permute-done((f32[1032,128]{1,0:T(8,128)S(1)}, f32[1032,128]{1,0:T(8,128)S(1)}, u32[]{:S(2)}, u32[]{:S(2)}) %collective-permute-start) | collective-permute-done | bytes 528416 | tf_op jit(solution)/shard_map/ppermute | solution.py:404
  18.4 1.3 %collective-permute-done.2.refs_4_.refs_12_ = f32[1032,128]{1,0:T(8,128)S(1)} collective-permute-done((f32[1032,128]{1,0:T(8,128)S(1)}, f32[1032,128]{1,0:T(8,128)S(1)}, u32[]{:S(2)}, u32[]{:S(2)}) %collective-permute-start.2) | collective-permute-done | bytes 528416 | tf_op jit(solution)/shard_map/ppermute | solution.py:399
  19.7 1.3 %collective-permute-start.4 = (f32[1032,128]{1,0:T(8,128)S(1)}, f32[1032,128]{1,0:T(8,128)}, u32[]{:S(2)}, u32[]{:S(2)}) collective-permute-start(f32[1032,128]{1,0:T(8,128)S(1)} %collective-permute-done.refs_1_.refs_2_), channel_id=1, source_target_pairs={{0,2},{2,4},{4,6},{6,0},{1,3},{3,5},{5,7},{7,1},{8,10},{10,12},{12... | collective-permute-start | bytes 1585160 | tf_op jit(solution)/shard_map/ppermute | solution.py:404
  21.0 1.2 collective-permute-start.5
  22.9 11.7 %collective-permute-done.4.refs_2_ = f32[1032,128]{1,0:T(8,128)} collective-permute-done((f32[1032,128]{1,0:T(8,128)S(1)}, f32[1032,128]{1,0:T(8,128)}, u32[]{:S(2)}, u32[]{:S(2)}) %collective-permute-start.4) | collective-permute-done | bytes 528416 | tf_op jit(solution)/shard_map/ppermute | solution.py:404
  34.6 1.3 %collective-permute-start.11 = (f32[1032,128]{1,0:T(8,128)S(1)}, f32[1032,128]{1,0:T(8,128)}, u32[]{:S(2)}, u32[]{:S(2)}) collective-permute-start(f32[1032,128]{1,0:T(8,128)S(1)} %collective-permute-done.refs_1_.refs_2_), channel_id=1, source_target_pairs={{0,16},{1,9},{8,24},{9,1},{16,0},{17,25},{24,8},{25,17},{2,18},{3,... | collective-permute-start | bytes 1585160 | tf_op jit(solution)/shard_map/ppermute | solution.py:399
  36.7 1.7 %collective-permute-start.12 = (f32[1032,128]{1,0:T(8,128)}, f32[1032,128]{1,0:T(8,128)S(1)}, u32[]{:S(2)}, u32[]{:S(2)}) collective-permute-start(f32[1032,128]{1,0:T(8,128)} %collective-permute-done.4.refs_2_), channel_id=1, source_target_pairs={{0,1},{1,0},{2,3},{3,2},{4,5},{5,4},{6,7},{7,6},{8,9},{9,8},{10,11... | collective-permute-start | bytes 1585160 | tf_op jit(solution)/shard_map/ppermute | solution.py:407
  38.5 6.8 %collective-permute-done.10.refs_3_ = f32[1032,128]{1,0:T(8,128)} collective-permute-done((f32[1032,128]{1,0:T(8,128)S(1)}, f32[1032,128]{1,0:T(8,128)}, u32[]{:S(2)}, u32[]{:S(2)}) %collective-permute-start.10) | collective-permute-done | bytes 528416 | tf_op jit(solution)/shard_map/ppermute | solution.py:399
  45.3 1.7 %collective-permute-done.11.refs_4_ = f32[1032,128]{1,0:T(8,128)} collective-permute-done((f32[1032,128]{1,0:T(8,128)S(1)}, f32[1032,128]{1,0:T(8,128)}, u32[]{:S(2)}, u32[]{:S(2)}) %collective-permute-start.11) | collective-permute-done | bytes 528416 | tf_op jit(solution)/shard_map/ppermute | solution.py:399
  47.0 6.6 %collective-permute-done.9.refs_3_.refs_2_ = f32[1032,128]{1,0:T(8,128)S(1)} collective-permute-done((f32[1032,128]{1,0:T(8,128)}, f32[1032,128]{1,0:T(8,128)S(1)}, u32[]{:S(2)}, u32[]{:S(2)}) %collective-permute-start.9) | collective-permute-done | bytes 528416 | tf_op jit(solution)/shard_map/ppermute | solution.py:404
  53.5 1.4 %collective-permute-start.17 = (f32[1032,128]{1,0:T(8,128)S(1)}, f32[1032,128]{1,0:T(8,128)S(1)}, u32[]{:S(2)}, u32[]{:S(2)}) collective-permute-start(f32[1032,128]{1,0:T(8,128)S(1)} %collective-permute-done.9.refs_3_.refs_2_), channel_id=1, source_target_pairs={{0,1},{1,0},{2,3},{3,2},{4,5},{5,4},{6,7},{7,6},{8,9},{9,8},{10,11... | collective-permute-start | bytes 1585160 | tf_op jit(solution)/shard_map/ppermute | solution.py:407
  54.9 1.7 %collective-permute-start.15 = (f32[1032,128]{1,0:T(8,128)}, f32[1032,128]{1,0:T(8,128)}, u32[]{:S(2)}, u32[]{:S(2)}) collective-permute-start(f32[1032,128]{1,0:T(8,128)} %collective-permute-done.4.refs_2_), channel_id=1, source_target_pairs={{0,8},{1,17},{8,0},{9,25},{16,24},{17,1},{24,16},{25,9},{2,10},{3,... | collective-permute-start | bytes 1585160 | tf_op jit(solution)/shard_map/ppermute | solution.py:399
  60.0 5.6 %left_panel.1 = (bf16[64,128,256]{2,1,0:T(8,128)(2,1)}, s32[180]{0:T(256)}) custom-call(s32[3]{0:T(128)} %pad_add_fusion.where_ref, f32[1032,128]{1,0:T(8,128)} %copy-done, f32[1032,128]{1,0:T(8,128)} %copy-done.8, f32[1032,128]{1,0:T(8,128)} %collective-permute-done.4.refs_2_, f32[1032,128]{1,0:T(8,128)} %copy-done.9, f32[1032,128]{1,0:T(8,128)} %copy-done.1, ...), custom_call_target="tpu_custom_call" | custom-call | tf_op jit(solution)/shard_map/left_panel/pallas_call | solution.py:121
  65.6 12.0 %tiles_0.1.refs_18_ = f32[768,1536]{1,0:T(8,128)} custom-call(s32[180]{0:T(256)} %get-tuple-element.77.refs_0_, bf16[64,128,256]{2,1,0:T(8,128)(2,1)} %get-tuple-element.78.refs_1_, f32[1032,128]{1,0:T(8,128)} %copy-done, f32[1032,128]{1,0:T(8,128)} %copy-done.2, f32[1032,128]{1,0:T(8,128)} %copy-done.3, f32[1032,128]{1,0:T(8,128)} %copy-done.4, ...), custom_call_target="tpu_custom_call" | custom-call | tf_op jit(solution)/shard_map/tiles_0/pallas_call | solution.py:358
  79.2 1.3 %collective-permute-start.22 = (f32[1032,128]{1,0:T(8,128)S(1)}, f32[1032,128]{1,0:T(8,128)S(1)}, u32[]{:S(2)}, u32[]{:S(2)}) collective-permute-start(f32[1032,128]{1,0:T(8,128)S(1)} %copy-done.10), channel_id=1, source_target_pairs={{0,16},{1,9},{8,24},{9,1},{16,0},{17,25},{24,8},{25,17},{2,18},{3,... | collective-permute-start | bytes 1585160 | tf_op jit(solution)/shard_map/ppermute | solution.py:399
  81.2 11.0 %tiles_1.1.refs_18_ = f32[768,1536]{1,0:T(8,128)} custom-call(s32[180]{0:T(256)} %get-tuple-element.77.refs_0_, bf16[64,128,256]{2,1,0:T(8,128)(2,1)} %get-tuple-element.78.refs_1_, f32[1032,128]{1,0:T(8,128)} %copy-done.8, f32[1032,128]{1,0:T(8,128)} %collective-permute-done.10.refs_3_, f32[1032,128]{1,0:T(8,128)} %collective-permute-done.11.refs_4_, ...), custom_call_target="tpu_custom_call" | custom-call | tf_op jit(solution)/shard_map/tiles_1/pallas_call | solution.py:358
  92.7 5.4 %collective-permute-done.20.refs_5_ = f32[1032,128]{1,0:T(8,128)S(1)} collective-permute-done((f32[1032,128]{1,0:T(8,128)}, f32[1032,128]{1,0:T(8,128)S(1)}, u32[]{:S(2)}, u32[]{:S(2)}) %collective-permute-start.20) | collective-permute-done | bytes 528416 | tf_op jit(solution)/shard_map/ppermute | solution.py:399
  99.2 1.7 %collective-permute-start.28 = (f32[1032,128]{1,0:T(8,128)S(1)}, f32[1032,128]{1,0:T(8,128)}, u32[]{:S(2)}, u32[]{:S(2)}) collective-permute-start(f32[1032,128]{1,0:T(8,128)S(1)} %collective-permute-done.21.refs_3_), channel_id=1, source_target_pairs={{0,17},{1,8},{8,25},{9,0},{16,1},{17,24},{24,9},{25,16},{2,19},{3,... | collective-permute-start | bytes 1585160 | tf_op jit(solution)/shard_map/ppermute | solution.py:399
  101.5 11.9 %tiles_2.1.refs_18_ = f32[768,1536]{1,0:T(8,128)} custom-call(s32[180]{0:T(256)} %get-tuple-element.77.refs_0_, bf16[64,128,256]{2,1,0:T(8,128)(2,1)} %get-tuple-element.78.refs_1_, f32[1032,128]{1,0:T(8,128)} %collective-permute-done.4.refs_2_, f32[1032,128]{1,0:T(8,128)} %collective-permute-done.15.refs_3_, f32[1032,128]{1,0:T(8,128)} %collective-permute-done.16.refs_4_, ...), custom_call_target="tpu_custom_call" | custom-call | tf_op jit(solution)/shard_map/tiles_2/pallas_call | solution.py:358
  114.2 10.2 %tiles_3.1 = f32[768,1536]{1,0:T(8,128)} custom-call(s32[180]{0:T(256)} %get-tuple-element.77.refs_0_, bf16[64,128,256]{2,1,0:T(8,128)(2,1)} %get-tuple-element.78.refs_1_, f32[1032,128]{1,0:T(8,128)} %copy-done.9, f32[1032,128]{1,0:T(8,128)} %copy-done.14, f32[1032,128]{1,0:T(8,128)} %copy-done.15, f32[1032,128]{1,0:T(8,128)} %copy-done.18, ...), custom_call_target="tpu_custom_call" | custom-call | tf_op jit(solution)/shard_map/tiles_3/pallas_call | solution.py:358
  (84 shorter events, 11.8 us)
Async XLA Ops:
  2.4 15.9 %collective-permute-start = (f32[1032,128]{1,0:T(8,128)S(1)}, f32[1032,128]{1,0:T(8,128)S(1)}, u32[]{:S(2)}, u32[]{:S(2)}) collective-permute-start(f32[1032,128]{1,0:T(8,128)S(1)} %select_maximum_fusion.refs_0_.refs_2_.refs_10_), channel_id=1, source_target_pairs={{0,2},{2,4},{4,6},{6,0},{1,3},{3,5},{5,7},{7,1},{8,10},{10,12},{12... | collective-permute-start | bytes 1585160 | tf_op jit(solution)/shard_map/ppermute | solution.py:404
  4.6 13.8 %collective-permute-start.1 = (f32[1032,128]{1,0:T(8,128)S(1)}, f32[1032,128]{1,0:T(8,128)S(1)}, u32[]{:S(2)}, u32[]{:S(2)}) collective-permute-start(f32[1032,128]{1,0:T(8,128)S(1)} %select_maximum_fusion.refs_0_.refs_2_.refs_10_), channel_id=1, source_target_pairs={{0,8},{1,17},{8,0},{9,25},{16,24},{17,1},{24,16},{25,9},{2,10},{3,... | collective-permute-start | bytes 1585160 | tf_op jit(solution)/shard_map/ppermute | solution.py:399
  5.8 13.9 %collective-permute-start.2 = (f32[1032,128]{1,0:T(8,128)S(1)}, f32[1032,128]{1,0:T(8,128)S(1)}, u32[]{:S(2)}, u32[]{:S(2)}) collective-permute-start(f32[1032,128]{1,0:T(8,128)S(1)} %select_maximum_fusion.refs_0_.refs_2_.refs_10_), channel_id=1, source_target_pairs={{0,16},{1,9},{8,24},{9,1},{16,0},{17,25},{24,8},{25,17},{2,18},{3,... | collective-permute-start | bytes 1585160 | tf_op jit(solution)/shard_map/ppermute | solution.py:399
  7.0 12.7 %collective-permute-start.3 = (f32[1032,128]{1,0:T(8,128)S(1)}, f32[1032,128]{1,0:T(8,128)S(1)}, u32[]{:S(2)}, u32[]{:S(2)}) collective-permute-start(f32[1032,128]{1,0:T(8,128)S(1)} %select_maximum_fusion.refs_0_.refs_2_.refs_10_), channel_id=1, source_target_pairs={{0,1},{1,0},{2,3},{3,2},{4,5},{5,4},{6,7},{7,6},{8,9},{9,8},{10,11... | collective-permute-start | bytes 1585160 | tf_op jit(solution)/shard_map/ppermute | solution.py:407
  19.7 14.9 %collective-permute-start.4 = (f32[1032,128]{1,0:T(8,128)S(1)}, f32[1032,128]{1,0:T(8,128)}, u32[]{:S(2)}, u32[]{:S(2)}) collective-permute-start(f32[1032,128]{1,0:T(8,128)S(1)} %collective-permute-done.refs_1_.refs_2_), channel_id=1, source_target_pairs={{0,2},{2,4},{4,6},{6,0},{1,3},{3,5},{5,7},{7,1},{8,10},{10,12},{12... | collective-permute-start | bytes 1585160 | tf_op jit(solution)/shard_map/ppermute | solution.py:404
  21.0 13.6 %collective-permute-start.5 = (f32[1032,128]{1,0:T(8,128)S(1)}, f32[1032,128]{1,0:T(8,128)S(1)}, u32[]{:S(2)}, u32[]{:S(2)}) collective-permute-start(f32[1032,128]{1,0:T(8,128)S(1)} %collective-permute-done.1.refs_3_.refs_11_), channel_id=1, source_target_pairs={{0,16},{1,9},{8,24},{9,1},{16,0},{17,25},{24,8},{25,17},{2,18},{3,... | collective-permute-start | bytes 1585160 | tf_op jit(solution)/shard_map/ppermute | solution.py:399
  22.3 13.7 %collective-permute-start.6 = (f32[1032,128]{1,0:T(8,128)S(1)}, f32[1032,128]{1,0:T(8,128)S(1)}, u32[]{:S(2)}, u32[]{:S(2)}) collective-permute-start(f32[1032,128]{1,0:T(8,128)S(1)} %collective-permute-done.refs_1_.refs_2_), channel_id=1, source_target_pairs={{0,1},{1,0},{2,3},{3,2},{4,5},{5,4},{6,7},{7,6},{8,9},{9,8},{10,11... | collective-permute-start | bytes 1585160 | tf_op jit(solution)/shard_map/ppermute | solution.py:407
  22.4 13.5 %collective-permute-start.7 = (f32[1032,128]{1,0:T(8,128)S(1)}, f32[1032,128]{1,0:T(8,128)S(1)}, u32[]{:S(2)}, u32[]{:S(2)}) collective-permute-start(f32[1032,128]{1,0:T(8,128)S(1)} %collective-permute-done.1.refs_3_.refs_11_), channel_id=1, source_target_pairs={{0,1},{1,0},{2,3},{3,2},{4,5},{5,4},{6,7},{7,6},{8,9},{9,8},{10,11... | collective-permute-start | bytes 1585160 | tf_op jit(solution)/shard_map/ppermute | solution.py:407
  22.8 13.2 %collective-permute-start.8 = (f32[1032,128]{1,0:T(8,128)S(1)}, f32[1032,128]{1,0:T(8,128)S(1)}, u32[]{:S(2)}, u32[]{:S(2)}) collective-permute-start(f32[1032,128]{1,0:T(8,128)S(1)} %collective-permute-done.2.refs_4_.refs_12_), channel_id=1, source_target_pairs={{0,1},{1,0},{2,3},{3,2},{4,5},{5,4},{6,7},{7,6},{8,9},{9,8},{10,11... | collective-permute-start | bytes 1585160 | tf_op jit(solution)/shard_map/ppermute | solution.py:407
  38.5 15.1 %collective-permute-start.9 = (f32[1032,128]{1,0:T(8,128)}, f32[1032,128]{1,0:T(8,128)S(1)}, u32[]{:S(2)}, u32[]{:S(2)}) collective-permute-start(f32[1032,128]{1,0:T(8,128)} %collective-permute-done.4.refs_2_), channel_id=1, source_target_pairs={{0,2},{2,4},{4,6},{6,0},{1,3},{3,5},{5,7},{7,1},{8,10},{10,12},{12... | collective-permute-start | bytes 1585160 | tf_op jit(solution)/shard_map/ppermute | solution.py:404
  54.9 22.7 %collective-permute-start.15 = (f32[1032,128]{1,0:T(8,128)}, f32[1032,128]{1,0:T(8,128)}, u32[]{:S(2)}, u32[]{:S(2)}) collective-permute-start(f32[1032,128]{1,0:T(8,128)} %collective-permute-done.4.refs_2_), channel_id=1, source_target_pairs={{0,8},{1,17},{8,0},{9,25},{16,24},{17,1},{24,16},{25,9},{2,10},{3,... | collective-permute-start | bytes 1585160 | tf_op jit(solution)/shard_map/ppermute | solution.py:399
  56.6 21.0 %collective-permute-start.16 = (f32[1032,128]{1,0:T(8,128)}, f32[1032,128]{1,0:T(8,128)}, u32[]{:S(2)}, u32[]{:S(2)}) collective-permute-start(f32[1032,128]{1,0:T(8,128)} %collective-permute-done.4.refs_2_), channel_id=1, source_target_pairs={{0,16},{1,9},{8,24},{9,1},{16,0},{17,25},{24,8},{25,17},{2,18},{3,... | collective-permute-start | bytes 1585160 | tf_op jit(solution)/shard_map/ppermute | solution.py:399
  56.9 20.8 %collective-permute-start.14 = (f32[1032,128]{1,0:T(8,128)}, f32[1032,128]{1,0:T(8,128)}, u32[]{:S(2)}, u32[]{:S(2)}) collective-permute-start(f32[1032,128]{1,0:T(8,128)} %collective-permute-done.10.refs_3_), channel_id=1, source_target_pairs={{0,16},{1,9},{8,24},{9,1},{16,0},{17,25},{24,8},{25,17},{2,18},{3,... | collective-permute-start | bytes 1585160 | tf_op jit(solution)/shard_map/ppermute | solution.py:399
  58.1 19.6 %collective-permute-start.18 = (f32[1032,128]{1,0:T(8,128)}, f32[1032,128]{1,0:T(8,128)}, u32[]{:S(2)}, u32[]{:S(2)}) collective-permute-start(f32[1032,128]{1,0:T(8,128)} %collective-permute-done.10.refs_3_), channel_id=1, source_target_pairs={{0,1},{1,0},{2,3},{3,2},{4,5},{5,4},{6,7},{7,6},{8,9},{9,8},{10,11... | collective-permute-start | bytes 1585160 | tf_op jit(solution)/shard_map/ppermute | solution.py:407
  58.9 18.8 %collective-permute-start.19 = (f32[1032,128]{1,0:T(8,128)}, f32[1032,128]{1,0:T(8,128)}, u32[]{:S(2)}, u32[]{:S(2)}) collective-permute-start(f32[1032,128]{1,0:T(8,128)} %collective-permute-done.11.refs_4_), channel_id=1, source_target_pairs={{0,1},{1,0},{2,3},{3,2},{4,5},{5,4},{6,7},{7,6},{8,9},{9,8},{10,11... | collective-permute-start | bytes 1585160 | tf_op jit(solution)/shard_map/ppermute | solution.py:407
  78.0 14.2 %collective-permute-start.21 = (f32[1032,128]{1,0:T(8,128)S(1)}, f32[1032,128]{1,0:T(8,128)S(1)}, u32[]{:S(2)}, u32[]{:S(2)}) collective-permute-start(f32[1032,128]{1,0:T(8,128)S(1)} %copy-done.10), channel_id=1, source_target_pairs={{0,8},{1,17},{8,0},{9,25},{16,24},{17,1},{24,16},{25,9},{2,10},{3,... | collective-permute-start | bytes 1585160 | tf_op jit(solution)/shard_map/ppermute | solution.py:399
  79.2 13.5 %collective-permute-start.22 = (f32[1032,128]{1,0:T(8,128)S(1)}, f32[1032,128]{1,0:T(8,128)S(1)}, u32[]{:S(2)}, u32[]{:S(2)}) collective-permute-start(f32[1032,128]{1,0:T(8,128)S(1)} %copy-done.10), channel_id=1, source_target_pairs={{0,16},{1,9},{8,24},{9,1},{16,0},{17,25},{24,8},{25,17},{2,18},{3,... | collective-permute-start | bytes 1585160 | tf_op jit(solution)/shard_map/ppermute | solution.py:399
  80.5 17.6 %collective-permute-start.20 = (f32[1032,128]{1,0:T(8,128)}, f32[1032,128]{1,0:T(8,128)S(1)}, u32[]{:S(2)}, u32[]{:S(2)}) collective-permute-start(f32[1032,128]{1,0:T(8,128)} %collective-permute-done.15.refs_3_), channel_id=1, source_target_pairs={{0,16},{1,9},{8,24},{9,1},{16,0},{17,25},{24,8},{25,17},{2,18},{3,... | collective-permute-start | bytes 1585160 | tf_op jit(solution)/shard_map/ppermute | solution.py:399
  80.6 17.5 %collective-permute-start.24 = (f32[1032,128]{1,0:T(8,128)}, f32[1032,128]{1,0:T(8,128)S(1)}, u32[]{:S(2)}, u32[]{:S(2)}) collective-permute-start(f32[1032,128]{1,0:T(8,128)} %collective-permute-done.15.refs_3_), channel_id=1, source_target_pairs={{0,1},{1,0},{2,3},{3,2},{4,5},{5,4},{6,7},{7,6},{8,9},{9,8},{10,11... | collective-permute-start | bytes 1585160 | tf_op jit(solution)/shard_map/ppermute | solution.py:407
  81.2 16.9 %collective-permute-start.25 = (f32[1032,128]{1,0:T(8,128)}, f32[1032,128]{1,0:T(8,128)}, u32[]{:S(2)}, u32[]{:S(2)}) collective-permute-start(f32[1032,128]{1,0:T(8,128)} %collective-permute-done.16.refs_4_), channel_id=1, source_target_pairs={{0,1},{1,0},{2,3},{3,2},{4,5},{5,4},{6,7},{7,6},{8,9},{9,8},{10,11... | collective-permute-start | bytes 1585160 | tf_op jit(solution)/shard_map/ppermute | solution.py:407
  98.2 15.2 %collective-permute-start.26 = (f32[1032,128]{1,0:T(8,128)S(1)}, f32[1032,128]{1,0:T(8,128)S(1)}, u32[]{:S(2)}, u32[]{:S(2)}) collective-permute-start(f32[1032,128]{1,0:T(8,128)S(1)} %collective-permute-done.21.refs_3_), channel_id=1, source_target_pairs={{0,16},{1,9},{8,24},{9,1},{16,0},{17,25},{24,8},{25,17},{2,18},{3,... | collective-permute-start | bytes 1585160 | tf_op jit(solution)/shard_map/ppermute | solution.py:399
  99.2 14.3 %collective-permute-start.28 = (f32[1032,128]{1,0:T(8,128)S(1)}, f32[1032,128]{1,0:T(8,128)}, u32[]{:S(2)}, u32[]{:S(2)}) collective-permute-start(f32[1032,128]{1,0:T(8,128)S(1)} %collective-permute-done.21.refs_3_), channel_id=1, source_target_pairs={{0,17},{1,8},{8,25},{9,0},{16,1},{17,24},{24,9},{25,16},{2,19},{3,... | collective-permute-start | bytes 1585160 | tf_op jit(solution)/shard_map/ppermute | solution.py:399
  100.9 12.5 %collective-permute-start.29 = (f32[1032,128]{1,0:T(8,128)S(1)}, f32[1032,128]{1,0:T(8,128)}, u32[]{:S(2)}, u32[]{:S(2)}) collective-permute-start(f32[1032,128]{1,0:T(8,128)S(1)} %collective-permute-done.21.refs_3_), channel_id=1, source_target_pairs={{0,1},{1,0},{2,3},{3,2},{4,5},{5,4},{6,7},{7,6},{8,9},{9,8},{10,11... | collective-permute-start | bytes 1585160 | tf_op jit(solution)/shard_map/ppermute | solution.py:407
  101.1 12.4 %collective-permute-start.30 = (f32[1032,128]{1,0:T(8,128)S(1)}, f32[1032,128]{1,0:T(8,128)}, u32[]{:S(2)}, u32[]{:S(2)}) collective-permute-start(f32[1032,128]{1,0:T(8,128)S(1)} %collective-permute-done.22.refs_4_), channel_id=1, source_target_pairs={{0,1},{1,0},{2,3},{3,2},{4,5},{5,4},{6,7},{7,6},{8,9},{9,8},{10,11... | collective-permute-start | bytes 1585160 | tf_op jit(solution)/shard_map/ppermute | solution.py:407
  (26 other events, 428.3 us)

commit v4 on v3

--- a/solution.py
+++ b/solution.py
@@ -9,12 +9,9 @@
 
 ROW_BLOCKS = 12
 GROUP = 4
-AHEAD = (0, 1, 2, 3)
-LATER = (0, 1, 1, 1)
 CUBES = 8
 CHUNK = 128
 STRIP = 384
-PANEL_MB = 61
 TILE_MB = 61
 AXES = ("row", "col", "layer")
 VMEM = pl.BlockSpec(memory_space=pltpu.VMEM)
@@ -67,18 +64,14 @@
     return my_row ^ jnp.where(layer == 0, first, second)
 
 
-def panel_kernel(sizes, segments, where_ref, *refs):
+def build_left(sizes, segments, where_ref, moves, buffer, lists, left, table):
     n_row, n_col, n_layer, listed, side = sizes
-    arrays = len(segments)
-    array_refs = refs[:arrays]
-    panel, table, buffer, lists, sem = refs[arrays:]
     nblk = ROW_BLOCKS * n_row
     cblk = nblk // n_col
     half = ROW_BLOCKS // n_layer
     my_col, my_layer = where_ref[1], where_ref[2]
-    moves = start_copies(side, listed, array_refs, buffer, lists, sem)
-    nxt, tag = nblk, nblk + arrays * listed
-    total = tag + arrays * listed
+    nxt, tag = nblk, nblk + left.shape[0]
+    total = tag + left.shape[0]
 
     def clear(i, _):
         table[i] = -1
@@ -103,8 +96,8 @@
                 table[key] = count
                 table[tag + count] = mark
                 high, low = split(buffer[lanes(i * listed + s, side), :])
-                panel[count, :, :side] = high
-                panel[count, :, side:] = low
+                left[count, :, :side] = high
+                left[count, :, side:] = low
 
             return count + use.astype(jnp.int32)
 
@@ -114,51 +107,44 @@
         table[total + 1 + i] = where_ref[i]
 
 
-def panel_call(sizes, segments, arrays, where):
-    n_row, n_col, n_layer, listed, side = sizes
-    nblk = ROW_BLOCKS * n_row
-    total = len(segments) * listed
-    return pl.pallas_call(
-        functools.partial(panel_kernel, sizes, segments),
-        out_shape=[
-            jax.ShapeDtypeStruct((total, side, 2 * side), jnp.bfloat16),
-            jax.ShapeDtypeStruct((nblk + 2 * total + 4,), jnp.int32),
-        ],
-        in_specs=[SMEM] + [HBM] * len(arrays),
-        out_specs=[VMEM, SMEM],
-        scratch_shapes=[
-            pltpu.VMEM((total * side, side), jnp.float32),
-            pltpu.SMEM((len(segments), side), jnp.float32),
-            pltpu.SemaphoreType.DMA((2, len(segments))),
-        ],
-        compiler_params=params(max(PANEL_MB, total // 4)),
-        name="left_panel",
-    )(where, *arrays)
-
-
-def tile_kernel(sizes, shifts, segments, *refs):
+def tile_kernel(sizes, shifts, segments, builds, *refs):
     n_row, n_col, n_layer, listed, side = sizes
     arrays = len(segments)
-    table, left_ref = refs[:2]
-    array_refs = refs[2 : 2 + arrays]
-    rest = refs[2 + arrays :]
+    if builds:
+        where_ref, array_refs = refs[0], refs[1 : 1 + arrays]
+        build_refs = refs[1 + arrays : 1 + arrays + len(builds)]
+        rest = refs[1 + arrays + len(builds) :]
+    else:
+        table, left_ref = refs[:2]
+        array_refs = refs[2 : 2 + arrays]
+        rest = refs[2 + arrays :]
     if shifts[0]:
         column_refs, before, rest = rest[: n_layer * 4], rest[n_layer * 4], rest[n_layer * 4 + 1 :]
     else:
         column_refs = array_refs
-    (out_hbm, buffer, lists, sem, left, left_sem, column, column_lists, column_sem) = rest[:9]
-    late, out_sem, out_ref, right, panel, square, wide, plan, cubes = rest[9:]
+    if builds:
+        out_hbm, left_ref, table, *rest, build_buffer, build_lists, build_sem = rest
+    else:
+        out_hbm, *rest = rest
+    (buffer, lists, sem, left, left_sem, column, column_lists, column_sem) = rest[:8]
+    late, out_sem, out_ref, right, panel, square, wide, plan, cubes = rest[8:]
     nblk = ROW_BLOCKS * n_row
     cblk = nblk // n_col
     rows = ROW_BLOCKS // n_layer * side
     pairs = n_layer * listed
     nxt, tag = nblk, nblk + left.shape[0]
     total = tag + left.shape[0]
-    my_row, my_col, my_layer = table[total + 1], table[total + 2], table[total + 3]
+    if builds:
+        my_row, my_col, my_layer = where_ref[0], where_ref[1], where_ref[2]
+        built = start_copies(side, listed, build_refs, build_buffer, build_lists, build_sem)
+    else:
+        my_row, my_col, my_layer = table[total + 1], table[total + 2], table[total + 3]
     moves = start_copies(side, listed, array_refs, buffer, lists, sem)
 
     def get_left(i):
         part = pl.ds(pl.multiple_of(i * listed, listed), listed)
+        if builds:
+            return pltpu.make_async_copy(left.at[part], left_ref.at[part], left_sem.at[i])
         return pltpu.make_async_copy(left_ref.at[part], left.at[part], left_sem.at[i])
 
     def each_left(step):
@@ -168,7 +154,8 @@
 
         lax.fori_loop(0, (table[total] + listed - 1) // listed, one, 0)
 
-    each_left(lambda copy: copy.start())
+    if not builds:
+        each_left(lambda copy: copy.start())
 
     cols = [lax.rem(my_col + (n_col - shift), n_col) for shift in shifts]
     meets = [col * cblk // ROW_BLOCKS for col in cols]
@@ -207,6 +194,10 @@
         get_before = pltpu.make_async_copy(before, out_ref, late)
         get_before.start()
 
+    if builds:
+        build_left(sizes, builds, where_ref, built, build_buffer, build_lists, left, table)
+        each_left(lambda copy: copy.start())
+
     for t, shift in enumerate(shifts):
 
         def zero(j, _):
@@ -267,7 +258,7 @@
                 square[j, at, :] = square[j, at, :] + parts[u]
             return 0
 
-        if not t:
+        if not t and not builds:
             each_left(lambda copy: copy.wait())
         lax.fori_loop(0, (count + GROUP - 1) // GROUP, group, 0)
         if not shift:
@@ -343,9 +334,11 @@
         return 0
 
     lax.fori_loop(0, rows // STRIP, written, 0)
-
-
-def tile_call(sizes, shifts, segments, arrays, lefts, column, before):
+    if builds:
+        each_left(lambda copy: copy.wait())
+
+
+def tile_call(sizes, shifts, segments, arrays, builds, built, where, lefts, column, before):
     n_row, n_col, n_layer, listed, side = sizes
     nblk = ROW_BLOCKS * n_row
     cblk = nblk // n_col
@@ -353,35 +346,50 @@
     rows = half * side
     total = len(segments) * listed
     pairs = n_layer * listed
-    left, table = lefts
+    lines = n_col * n_layer * listed
+    out = jax.ShapeDtypeStruct((rows, cblk * side), jnp.float32)
+    left = jax.ShapeDtypeStruct((lines, side, 2 * side), jnp.bfloat16)
+    table = jax.ShapeDtypeStruct((nblk + 2 * lines + 4,), jnp.int32)
     extra = [] if before is None else [*column, before]
-    return pl.pallas_call(
-        functools.partial(tile_kernel, sizes, shifts, segments),
-        out_shape=jax.ShapeDtypeStruct((rows, cblk * side), jnp.float32),
-        in_specs=[SMEM] + [HBM] * (1 + len(arrays) + len(extra)),
-        out_specs=HBM,
-        scratch_shapes=[
-            pltpu.VMEM((total * side, side), jnp.float32),
-            pltpu.SMEM((len(segments), side), jnp.float32),
-            pltpu.SemaphoreType.DMA((2, len(segments))),
-            pltpu.VMEM(left.shape, left.dtype),
-            pltpu.SemaphoreType.DMA((left.shape[0] // listed,)),
-            pltpu.VMEM((len(shifts) * pairs * side, side), jnp.float32),
-            pltpu.SMEM((len(shifts) * n_layer, side), jnp.float32),
-            pltpu.SemaphoreType.DMA((2, len(shifts) * n_layer)),
-            pltpu.SemaphoreType.DMA,
-            pltpu.SemaphoreType.DMA((rows // STRIP,)),
-            pltpu.VMEM((rows, cblk * side), jnp.float32),
-            pltpu.VMEM((total, side, 2 * side), jnp.bfloat16),
-            pltpu.VMEM((pairs, side, 2 * side), jnp.bfloat16),
-            pltpu.VMEM((cblk + 1, rows, side), jnp.float32),
-            pltpu.VMEM((cblk + 1, rows, 2 * side), jnp.bfloat16),
-            pltpu.SMEM((4, total * half + GROUP), jnp.int32),
-            pltpu.SMEM((3, pairs + CUBES), jnp.int32),
-        ],
+    scratch = [
+        pltpu.VMEM((total * side, side), jnp.float32),
+        pltpu.SMEM((len(segments), side), jnp.float32),
+        pltpu.SemaphoreType.DMA((2, len(segments))),
+        pltpu.VMEM(left.shape, left.dtype),
+        pltpu.SemaphoreType.DMA((lines // listed,)),
+        pltpu.VMEM((len(shifts) * pairs * side, side), jnp.float32),
+        pltpu.SMEM((len(shifts) * n_layer, side), jnp.float32),
+        pltpu.SemaphoreType.DMA((2, len(shifts) * n_layer)),
+        pltpu.SemaphoreType.DMA,
+        pltpu.SemaphoreType.DMA((rows // STRIP,)),
+        pltpu.VMEM((rows, cblk * side), jnp.float32),
+        pltpu.VMEM((total, side, 2 * side), jnp.bfloat16),
+        pltpu.VMEM((pairs, side, 2 * side), jnp.bfloat16),
+        pltpu.VMEM((cblk + 1, rows, side), jnp.float32),
+        pltpu.VMEM((cblk + 1, rows, 2 * side), jnp.bfloat16),
+        pltpu.SMEM((4, total * half + GROUP), jnp.int32),
+        pltpu.SMEM((3, pairs + CUBES), jnp.int32),
+    ]
+    if builds:
+        scratch += [
+            pltpu.VMEM((lines * side, side), jnp.float32),
+            pltpu.SMEM((len(builds), side), jnp.float32),
+            pltpu.SemaphoreType.DMA((2, len(builds))),
+        ]
+    call = pl.pallas_call(
+        functools.partial(tile_kernel, sizes, shifts, segments, builds),
+        out_shape=[out, left, table] if builds else out,
+        in_specs=[SMEM] + [HBM] * (len(arrays) + len(extra) + (len(built) if builds else 1)),
+        out_specs=[HBM, HBM, SMEM] if builds else HBM,
+        scratch_shapes=scratch,
         compiler_params=params(TILE_MB),
         name="tiles_" + "_".join(str(s) for s in shifts),
-    )(table, left, *arrays, *extra)
+    )
+    if builds:
+        out, left, table = call(where, *arrays, *built)
+        return out, (left, table)
+    left, table = lefts
+    return call(table, left, *arrays, *extra), lefts
 
 
 def shards(blocks, block_ids, counts):
@@ -427,24 +435,35 @@
     def quads(shifts):
         return [(k, s) for s in shifts for k in ways]
 
-    def tiles(shifts, total):
+    def tiles(shifts, total, lefts):
         for i in range(0, len(shifts), 2):
             segments, arrays = gathered(quads(shifts[i : i + 2]))
+            builds, built = [], []
+            if lefts is None:
+                builds, built = gathered([("A", s) for s in range(n_col)])
             column = gathered(quads([0]))[1]
-            total = tile_call(
-                sizes, tuple(shifts[i : i + 2]), segments, arrays, lefts, column, total
+            total, lefts = tile_call(
+                sizes,
+                tuple(shifts[i : i + 2]),
+                segments,
+                arrays,
+                builds,
+                built,
+                where,
+                lefts,
+                column,
+                total,
             )
-        return total
-
-    rounds = [[] for _ in range(2 * n_col)]
+        return total, lefts
+
+    rounds = [[] for _ in range(n_col + 3)]
     for s in range(n_col):
         if s:
-            rounds[s - 1].append((("A", s), s - 1))
-        first = AHEAD[min(s, 3)] + max(0, s - 3)
-        there = first + LATER[min(s, 3)]
-        rounds[first] += [(("U", s), there), (("V", s), there)]
-        rounds[there + 1].append((("D", s), there + 1))
-    last = max(t for t in range(2 * n_col) if rounds[t])
+            rounds[s - 1].append(("A", s))
+        rounds[s].append(("U", s))
+        rounds[s + min(s, 1)].append(("V", s))
+        rounds[s + min(s, 1) + 1].append(("D", s))
+    last = max(t for t in range(n_col + 3) if rounds[t])
     makers = {
         "A": lambda s: ring(held[("A", s - 1)]),
         "U": lambda s: across(held[("A", s)]),
@@ -452,24 +471,20 @@
         "D": lambda s: along(held[("U", s)]),
     }
     done = 0
-    flying = {}
     for t in range(last + 2):
-        for name, there in rounds[t]:
-            flying[name] = (makers[name[0]](name[1]), there)
+        sent = {}
+        for name in rounds[t] if t <= last else []:
+            sent[name] = makers[name[0]](name[1])
             if t == last:
                 twin[name] = beside(held[("U", name[1])])
         twin.update({name: sibling(held[name]) for name in fresh if name not in twin})
-        if lefts is None and ("A", n_col - 1) in twin:
-            segments, arrays = gathered([("A", s) for s in range(n_col)])
-            lefts = panel_call(sizes, segments, arrays, where)
         ready = done
-        while lefts is not None and ready < n_col and {("D", ready)} <= held.keys() & twin.keys():
+        while ("A", n_col - 1) in twin and ready < n_col and {("D", ready)} <= held.keys() & twin.keys():
             ready += 1
-        total = tiles(list(range(done, ready)), total)
+        total, lefts = tiles(list(range(done, ready)), total, lefts)
         done = ready
         if t > last:
             return total
-        sent = {n: flying.pop(n)[0] for n in list(flying) if flying[n][1] == t}
         copied = {n: twin[n] for n in [*fresh, *sent] if n in twin}
         sent, copied, lefts, total = lax.optimization_barrier((sent, copied, lefts, total))
         held.update(sent)

time: 127 us -> 118 us (0.929); the launches traced: 124 us -> 117 us
  waiting for transfers between devices: 43.7 us -> 33.3 us
  starting transfers between devices: 24.3 us -> 29.5 us
    ppermute x15, starting transfers between devices: 7.35 us -> 16.9 us  [sibling(): lax.ppermute(y, 'layer', [(i, n_layer - 1 - i) for i in range(n_layer)])]
    ppermute x3, waiting for transfers between devices: 28 us -> 22.4 us  [ring(): return lax.ppermute(y, 'col', [(i, (i + 1) % n_col) for i in range(n_col)])]
    ppermute x13, waiting for transfers between devices: 15.6 us -> 10.2 us  [flip(): return lambda y: lax.ppermute(y, ('row', 'layer'), pairs)]
    ppermute x13, starting transfers between devices: 13.4 us -> 9.07 us  [flip(): return lambda y: lax.ppermute(y, ('row', 'layer'), pairs)]
    pallas_call x5 -> x4, Pallas kernels: 50.7 us -> 49.5 us  [the longest x3 33.9 us: tile_call(): return (call(table, left, *arrays, *extra), lefts)]
  transfers between devices with their start and end apart: 31 -> 31, of which waited for: 8 -> 9; matrix products, arithmetic and copies ran while one was open for 0% -> 1% of each run, Pallas kernels for 33% -> 33%
where the time goes in v4:
time: 118 us; the launch traced here: 117 us
  Pallas kernels  49.5 us (42%)
  waiting for transfers between devices  33.3 us (28%)
  starting transfers between devices  29.5 us (25%)
  other arithmetic  2.36 us (2%)
  local copies, waits for them, and re-layouts  1.37 us (1%)
    pallas_call x3, Pallas kernels, tile_call(): return (call(table, left, *arrays, *extra), lefts)  33.9 us
    ppermute x3, waiting for transfers between devices, ring(): return lax.ppermute(y, 'col', [(i, (i + 1) % n_col) for i in range(n_col)])  22.4 us
    ppermute x15, starting transfers between devices, sibling(): lax.ppermute(y, 'layer', [(i, n_layer - 1 - i) for i in range(n_layer)])  16.9 us
    pallas_call x1, Pallas kernels, tile_call(): out, left, table = call(where, *arrays, *built)  15.6 us
    ppermute x13, waiting for transfers between devices, flip(): return lambda y: lax.ppermute(y, ('row', 'layer'), pairs)  10.2 us
    ppermute x13, starting transfers between devices, flip(): return lambda y: lax.ppermute(y, ('row', 'layer'), pairs)  9.07 us
    ppermute x3, starting transfers between devices, ring(): return lax.ppermute(y, 'col', [(i, (i + 1) % n_col) for i in range(n_col)])  3.53 us
  transfers between devices with their start and end apart: 31, of which 9 were waited for; matrix products, arithmetic and copies ran while one was open for 1% of the time, Pallas kernels for 33%

profile of v4, /device:TPU:1, one launch (start us, length us, event | category | flops | bytes accessed | tf_op | source)
XLA Modules:
  0.0 117.0 jit_solution(12090092961872658440)
XLA Ops:
  2.4 2.2 %collective-permute-start = (f32[1032,128]{1,0:T(8,128)S(1)}, f32[1032,128]{1,0:T(8,128)S(1)}, u32[]{:S(2)}, u32[]{:S(2)}) collective-permute-start(f32[1032,128]{1,0:T(8,128)S(1)} %select_maximum_fusion.refs_1_.refs_9_.refs_10_), channel_id=1, source_target_pairs={{0,2},{2,4},{4,6},{6,0},{1,3},{3,5},{5,7},{7,1},{8,10},{10,12},{12... | collective-permute-start | bytes 1585160 | tf_op jit(solution)/shard_map/ppermute | solution.py:412
  4.6 1.2 %collective-permute-start.1 = (f32[1032,128]{1,0:T(8,128)S(1)}, f32[1032,128]{1,0:T(8,128)S(1)}, u32[]{:S(2)}, u32[]{:S(2)}) collective-permute-start(f32[1032,128]{1,0:T(8,128)S(1)} %select_maximum_fusion.refs_1_.refs_9_.refs_10_), channel_id=1, source_target_pairs={{0,8},{1,17},{8,0},{9,25},{16,24},{17,1},{24,16},{25,9},{2,10},{3,... | collective-permute-start | bytes 1585160 | tf_op jit(solution)/shard_map/ppermute | solution.py:407
  5.8 1.2 %collective-permute-start.2 = (f32[1032,128]{1,0:T(8,128)S(1)}, f32[1032,128]{1,0:T(8,128)S(1)}, u32[]{:S(2)}, u32[]{:S(2)}) collective-permute-start(f32[1032,128]{1,0:T(8,128)S(1)} %select_maximum_fusion.refs_1_.refs_9_.refs_10_), channel_id=1, source_target_pairs={{0,16},{1,9},{8,24},{9,1},{16,0},{17,25},{24,8},{25,17},{2,18},{3,... | collective-permute-start | bytes 1585160 | tf_op jit(solution)/shard_map/ppermute | solution.py:407
  7.0 1.5 %collective-permute-start.3 = (f32[1032,128]{1,0:T(8,128)S(1)}, f32[1032,128]{1,0:T(8,128)S(1)}, u32[]{:S(2)}, u32[]{:S(2)}) collective-permute-start(f32[1032,128]{1,0:T(8,128)S(1)} %select_maximum_fusion.refs_1_.refs_9_.refs_10_), channel_id=1, source_target_pairs={{0,1},{1,0},{2,3},{3,2},{4,5},{5,4},{6,7},{7,6},{8,9},{9,8},{10,11... | collective-permute-start | bytes 1585160 | tf_op jit(solution)/shard_map/ppermute | solution.py:415
  8.6 9.8 %collective-permute-done.refs_10_.refs_2_ = f32[1032,128]{1,0:T(8,128)S(1)} collective-permute-done((f32[1032,128]{1,0:T(8,128)S(1)}, f32[1032,128]{1,0:T(8,128)S(1)}, u32[]{:S(2)}, u32[]{:S(2)}) %collective-permute-start) | collective-permute-done | bytes 528416 | tf_op jit(solution)/shard_map/ppermute | solution.py:412
  18.4 1.3 %collective-permute-done.2.refs_3_.refs_12_ = f32[1032,128]{1,0:T(8,128)S(1)} collective-permute-done((f32[1032,128]{1,0:T(8,128)S(1)}, f32[1032,128]{1,0:T(8,128)S(1)}, u32[]{:S(2)}, u32[]{:S(2)}) %collective-permute-start.2) | collective-permute-done | bytes 528416 | tf_op jit(solution)/shard_map/ppermute | solution.py:407
  19.7 1.3 %collective-permute-start.4 = (f32[1032,128]{1,0:T(8,128)S(1)}, f32[1032,128]{1,0:T(8,128)}, u32[]{:S(2)}, u32[]{:S(2)}) collective-permute-start(f32[1032,128]{1,0:T(8,128)S(1)} %collective-permute-done.refs_10_.refs_2_), channel_id=1, source_target_pairs={{0,2},{2,4},{4,6},{6,0},{1,3},{3,5},{5,7},{7,1},{8,10},{10,12},{12... | collective-permute-start | bytes 1585160 | tf_op jit(solution)/shard_map/ppermute | solution.py:412
  22.3 1.7 %collective-permute-start.7 = (f32[1032,128]{1,0:T(8,128)S(1)}, f32[1032,128]{1,0:T(8,128)S(1)}, u32[]{:S(2)}, u32[]{:S(2)}) collective-permute-start(f32[1032,128]{1,0:T(8,128)S(1)} %collective-permute-done.refs_10_.refs_2_), channel_id=1, source_target_pairs={{0,1},{1,0},{2,3},{3,2},{4,5},{5,4},{6,7},{7,6},{8,9},{9,8},{10,11... | collective-permute-start | bytes 1585160 | tf_op jit(solution)/shard_map/ppermute | solution.py:415
  23.9 10.7 %collective-permute-done.4.refs_11_.refs_2_ = f32[1032,128]{1,0:T(8,128)} collective-permute-done((f32[1032,128]{1,0:T(8,128)S(1)}, f32[1032,128]{1,0:T(8,128)}, u32[]{:S(2)}, u32[]{:S(2)}) %collective-permute-start.4) | collective-permute-done | bytes 528416 | tf_op jit(solution)/shard_map/ppermute | solution.py:412
  34.6 1.5 %collective-permute-start.9 = (f32[1032,128]{1,0:T(8,128)S(1)}, f32[1032,128]{1,0:T(8,128)S(1)}, u32[]{:S(2)}, u32[]{:S(2)}) collective-permute-start(f32[1032,128]{1,0:T(8,128)S(1)} %collective-permute-done.2.refs_3_.refs_12_), channel_id=1, source_target_pairs={{0,1},{1,0},{2,3},{3,2},{4,5},{5,4},{6,7},{7,6},{8,9},{9,8},{10,11... | collective-permute-start | bytes 1585160 | tf_op jit(solution)/shard_map/ppermute | solution.py:415
  36.1 1.2 %collective-permute-start.13 = (f32[1032,128]{1,0:T(8,128)S(1)}, f32[1032,128]{1,0:T(8,128)}, u32[]{:S(2)}, u32[]{:S(2)}) collective-permute-start(f32[1032,128]{1,0:T(8,128)S(1)} %collective-permute-done.refs_10_.refs_2_), channel_id=1, source_target_pairs={{0,16},{1,9},{8,24},{9,1},{16,0},{17,25},{24,8},{25,17},{2,18},{3,... | collective-permute-start | bytes 1585160 | tf_op jit(solution)/shard_map/ppermute | solution.py:407
  38.1 1.4 %collective-permute-start.14 = (f32[1032,128]{1,0:T(8,128)}, f32[1032,128]{1,0:T(8,128)S(1)}, u32[]{:S(2)}, u32[]{:S(2)}) collective-permute-start(f32[1032,128]{1,0:T(8,128)} %collective-permute-done.4.refs_11_.refs_2_), channel_id=1, source_target_pairs={{0,1},{1,0},{2,3},{3,2},{4,5},{5,4},{6,7},{7,6},{8,9},{9,8},{10,11... | collective-permute-start | bytes 1585160 | tf_op jit(solution)/shard_map/ppermute | solution.py:415
  39.5 7.4 %collective-permute-done.13.refs_4_ = f32[1032,128]{1,0:T(8,128)} collective-permute-done((f32[1032,128]{1,0:T(8,128)S(1)}, f32[1032,128]{1,0:T(8,128)}, u32[]{:S(2)}, u32[]{:S(2)}) %collective-permute-start.13) | collective-permute-done | bytes 528416 | tf_op jit(solution)/shard_map/ppermute | solution.py:407
  46.9 4.1 %collective-permute-start.16 = (f32[1032,128]{1,0:T(8,128)}, f32[1032,128]{1,0:T(8,128)S(1)}, u32[]{:S(2)}, u32[]{:S(2)}) collective-permute-start(f32[1032,128]{1,0:T(8,128)} %collective-permute-done.6.refs_3_), channel_id=1, source_target_pairs={{0,1},{1,0},{2,3},{3,2},{4,5},{5,4},{6,7},{7,6},{8,9},{9,8},{10,11... | collective-permute-start | bytes 1585160 | tf_op jit(solution)/shard_map/ppermute | solution.py:415
  51.0 1.9 %collective-permute-done.11.refs_12_.refs_2_ = f32[1032,128]{1,0:T(8,128)} collective-permute-done((f32[1032,128]{1,0:T(8,128)}, f32[1032,128]{1,0:T(8,128)}, u32[]{:S(2)}, u32[]{:S(2)}) %collective-permute-start.11) | collective-permute-done | bytes 528416 | tf_op jit(solution)/shard_map/ppermute | solution.py:412
  53.0 1.3 %collective-permute-start.19 = (f32[1032,128]{1,0:T(8,128)}, f32[1032,128]{1,0:T(8,128)}, u32[]{:S(2)}, u32[]{:S(2)}) collective-permute-start(f32[1032,128]{1,0:T(8,128)} %collective-permute-done.11.refs_12_.refs_2_), channel_id=1, source_target_pairs={{0,1},{1,0},{2,3},{3,2},{4,5},{5,4},{6,7},{7,6},{8,9},{9,8},{10,11... | collective-permute-start | bytes 1585160 | tf_op jit(solution)/shard_map/ppermute | solution.py:415
  54.3 1.2 %collective-permute-start.10 = (f32[1032,128]{1,0:T(8,128)}, f32[1032,128]{1,0:T(8,128)}, u32[]{:S(2)}, u32[]{:S(2)}) collective-permute-start(f32[1032,128]{1,0:T(8,128)} %collective-permute-done.6.refs_3_), channel_id=1, source_target_pairs={{0,16},{1,9},{8,24},{9,1},{16,0},{17,25},{24,8},{25,17},{2,18},{3,... | collective-permute-start | bytes 1585160 | tf_op jit(solution)/shard_map/ppermute | solution.py:407
  55.8 2.8 %collective-permute-start.20 = (f32[1032,128]{1,0:T(8,128)}, f32[1032,128]{1,0:T(8,128)}, u32[]{:S(2)}, u32[]{:S(2)}) collective-permute-start(f32[1032,128]{1,0:T(8,128)} %collective-permute-done.12.refs_3_), channel_id=1, source_target_pairs={{0,1},{1,0},{2,3},{3,2},{4,5},{5,4},{6,7},{7,6},{8,9},{9,8},{10,11... | collective-permute-start | bytes 1585160 | tf_op jit(solution)/shard_map/ppermute | solution.py:415
  59.3 15.6 %tiles_0.1 = (f32[768,1536]{1,0:T(8,128)}, bf16[64,128,256]{2,1,0:T(8,128)(2,1)}, s32[180]{0:T(256)}) custom-call(s32[3]{0:T(128)} %pad_add_fusion.refs_0_, f32[1032,128]{1,0:T(8,128)} %copy-done, f32[1032,128]{1,0:T(8,128)} %copy-done.2, f32[1032,128]{1,0:T(8,128)} %copy-done.3, f32[1032,128]{1,0:T(8,128)} %copy-done.4, f32[1032,128]{1,0:T(8,128)} %copy-done.1, ...), custom_call_target="tpu_custom_call" | custom-call | tf_op jit(solution)/shard_map/tiles_0/pallas_call | solution.py:389
  76.0 1.2 %collective-permute-start.23 = (f32[1032,128]{1,0:T(8,128)}, f32[1032,128]{1,0:T(8,128)S(1)}, u32[]{:S(2)}, u32[]{:S(2)}) collective-permute-start(f32[1032,128]{1,0:T(8,128)} %collective-permute-done.12.refs_3_), channel_id=1, source_target_pairs={{0,16},{1,9},{8,24},{9,1},{16,0},{17,25},{24,8},{25,17},{2,18},{3,... | collective-permute-start | bytes 1585160 | tf_op jit(solution)/shard_map/ppermute | solution.py:407
  78.9 11.0 %tiles_1.1.refs_18_ = f32[768,1536]{1,0:T(8,128)} custom-call(s32[180]{0:T(256)} %get-tuple-element.79.refs_0_, bf16[64,128,256]{2,1,0:T(8,128)(2,1)} %get-tuple-element.80.refs_1_, f32[1032,128]{1,0:T(8,128)} %copy-done.8, f32[1032,128]{1,0:T(8,128)} %collective-permute-done.6.refs_3_, f32[1032,128]{1,0:T(8,128)} %collective-permute-done.13.refs_4_, ...), custom_call_target="tpu_custom_call" | custom-call | tf_op jit(solution)/shard_map/tiles_1/pallas_call | solution.py:392
  91.2 1.2 %collective-permute-start.22 = (f32[1032,128]{1,0:T(8,128)}, f32[1032,128]{1,0:T(8,128)S(1)}, u32[]{:S(2)}, u32[]{:S(2)}) collective-permute-start(f32[1032,128]{1,0:T(8,128)} %collective-permute-done.17.refs_3_), channel_id=1, source_target_pairs={{0,16},{1,9},{8,24},{9,1},{16,0},{17,25},{24,8},{25,17},{2,18},{3,... | collective-permute-start | bytes 1585160 | tf_op jit(solution)/shard_map/ppermute | solution.py:407
  92.9 11.7 %tiles_2.1.refs_18_ = f32[768,1536]{1,0:T(8,128)} custom-call(s32[180]{0:T(256)} %get-tuple-element.79.refs_0_, bf16[64,128,256]{2,1,0:T(8,128)(2,1)} %get-tuple-element.80.refs_1_, f32[1032,128]{1,0:T(8,128)} %collective-permute-done.4.refs_11_.refs_2_, f32[1032,128]{1,0:T(8,128)} %collective-permute-done.12.refs_3_, ...), custom_call_target="tpu_custom_call" | custom-call | tf_op jit(solution)/shard_map/tiles_2/pallas_call | solution.py:392
  105.8 11.2 %tiles_3.1 = f32[768,1536]{1,0:T(8,128)} custom-call(s32[180]{0:T(256)} %get-tuple-element.79.refs_0_, bf16[64,128,256]{2,1,0:T(8,128)(2,1)} %get-tuple-element.80.refs_1_, f32[1032,128]{1,0:T(8,128)} %collective-permute-done.11.refs_12_.refs_2_, f32[1032,128]{1,0:T(8,128)} %collective-permute-done.17.refs_3_, f32[1032,128]{1,0:T(8,128)} %copy-done.12, ...), custom_call_target="tpu_custom_call" | custom-call | tf_op jit(solution)/shard_map/tiles_3/pallas_call | solution.py:392
  (81 shorter events, 10.5 us)
Async XLA Ops:
  2.4 15.9 %collective-permute-start = (f32[1032,128]{1,0:T(8,128)S(1)}, f32[1032,128]{1,0:T(8,128)S(1)}, u32[]{:S(2)}, u32[]{:S(2)}) collective-permute-start(f32[1032,128]{1,0:T(8,128)S(1)} %select_maximum_fusion.refs_1_.refs_9_.refs_10_), channel_id=1, source_target_pairs={{0,2},{2,4},{4,6},{6,0},{1,3},{3,5},{5,7},{7,1},{8,10},{10,12},{12... | collective-permute-start | bytes 1585160 | tf_op jit(solution)/shard_map/ppermute | solution.py:412
  4.6 13.8 %collective-permute-start.1 = (f32[1032,128]{1,0:T(8,128)S(1)}, f32[1032,128]{1,0:T(8,128)S(1)}, u32[]{:S(2)}, u32[]{:S(2)}) collective-permute-start(f32[1032,128]{1,0:T(8,128)S(1)} %select_maximum_fusion.refs_1_.refs_9_.refs_10_), channel_id=1, source_target_pairs={{0,8},{1,17},{8,0},{9,25},{16,24},{17,1},{24,16},{25,9},{2,10},{3,... | collective-permute-start | bytes 1585160 | tf_op jit(solution)/shard_map/ppermute | solution.py:407
  5.8 13.9 %collective-permute-start.2 = (f32[1032,128]{1,0:T(8,128)S(1)}, f32[1032,128]{1,0:T(8,128)S(1)}, u32[]{:S(2)}, u32[]{:S(2)}) collective-permute-start(f32[1032,128]{1,0:T(8,128)S(1)} %select_maximum_fusion.refs_1_.refs_9_.refs_10_), channel_id=1, source_target_pairs={{0,16},{1,9},{8,24},{9,1},{16,0},{17,25},{24,8},{25,17},{2,18},{3,... | collective-permute-start | bytes 1585160 | tf_op jit(solution)/shard_map/ppermute | solution.py:407
  7.0 12.7 %collective-permute-start.3 = (f32[1032,128]{1,0:T(8,128)S(1)}, f32[1032,128]{1,0:T(8,128)S(1)}, u32[]{:S(2)}, u32[]{:S(2)}) collective-permute-start(f32[1032,128]{1,0:T(8,128)S(1)} %select_maximum_fusion.refs_1_.refs_9_.refs_10_), channel_id=1, source_target_pairs={{0,1},{1,0},{2,3},{3,2},{4,5},{5,4},{6,7},{7,6},{8,9},{9,8},{10,11... | collective-permute-start | bytes 1585160 | tf_op jit(solution)/shard_map/ppermute | solution.py:415
  19.7 14.9 %collective-permute-start.4 = (f32[1032,128]{1,0:T(8,128)S(1)}, f32[1032,128]{1,0:T(8,128)}, u32[]{:S(2)}, u32[]{:S(2)}) collective-permute-start(f32[1032,128]{1,0:T(8,128)S(1)} %collective-permute-done.refs_10_.refs_2_), channel_id=1, source_target_pairs={{0,2},{2,4},{4,6},{6,0},{1,3},{3,5},{5,7},{7,1},{8,10},{10,12},{12... | collective-permute-start | bytes 1585160 | tf_op jit(solution)/shard_map/ppermute | solution.py:412
  21.0 15.0 %collective-permute-start.5 = (f32[1032,128]{1,0:T(8,128)S(1)}, f32[1032,128]{1,0:T(8,128)S(1)}, u32[]{:S(2)}, u32[]{:S(2)}) collective-permute-start(f32[1032,128]{1,0:T(8,128)S(1)} %collective-permute-done.1.refs_2_.refs_11_), channel_id=1, source_target_pairs={{0,16},{1,9},{8,24},{9,1},{16,0},{17,25},{24,8},{25,17},{2,18},{3,... | collective-permute-start | bytes 1585160 | tf_op jit(solution)/shard_map/ppermute | solution.py:407
  22.3 15.0 %collective-permute-start.6 = (f32[1032,128]{1,0:T(8,128)S(1)}, f32[1032,128]{1,0:T(8,128)}, u32[]{:S(2)}, u32[]{:S(2)}) collective-permute-start(f32[1032,128]{1,0:T(8,128)S(1)} %collective-permute-done.refs_10_.refs_2_), channel_id=1, source_target_pairs={{0,8},{1,17},{8,0},{9,25},{16,24},{17,1},{24,16},{25,9},{2,10},{3,... | collective-permute-start | bytes 1585160 | tf_op jit(solution)/shard_map/ppermute | solution.py:407
  22.3 15.0 %collective-permute-start.7 = (f32[1032,128]{1,0:T(8,128)S(1)}, f32[1032,128]{1,0:T(8,128)S(1)}, u32[]{:S(2)}, u32[]{:S(2)}) collective-permute-start(f32[1032,128]{1,0:T(8,128)S(1)} %collective-permute-done.refs_10_.refs_2_), channel_id=1, source_target_pairs={{0,1},{1,0},{2,3},{3,2},{4,5},{5,4},{6,7},{7,6},{8,9},{9,8},{10,11... | collective-permute-start | bytes 1585160 | tf_op jit(solution)/shard_map/ppermute | solution.py:415
  23.9 13.4 %collective-permute-start.8 = (f32[1032,128]{1,0:T(8,128)S(1)}, f32[1032,128]{1,0:T(8,128)S(1)}, u32[]{:S(2)}, u32[]{:S(2)}) collective-permute-start(f32[1032,128]{1,0:T(8,128)S(1)} %collective-permute-done.1.refs_2_.refs_11_), channel_id=1, source_target_pairs={{0,1},{1,0},{2,3},{3,2},{4,5},{5,4},{6,7},{7,6},{8,9},{9,8},{10,11... | collective-permute-start | bytes 1585160 | tf_op jit(solution)/shard_map/ppermute | solution.py:415
  37.6 15.3 %collective-permute-start.11 = (f32[1032,128]{1,0:T(8,128)}, f32[1032,128]{1,0:T(8,128)}, u32[]{:S(2)}, u32[]{:S(2)}) collective-permute-start(f32[1032,128]{1,0:T(8,128)} %collective-permute-done.4.refs_11_.refs_2_), channel_id=1, source_target_pairs={{0,2},{2,4},{4,6},{6,0},{1,3},{3,5},{5,7},{7,1},{8,10},{10,12},{12... | collective-permute-start | bytes 1585160 | tf_op jit(solution)/shard_map/ppermute | solution.py:412
  37.6 15.3 %collective-permute-start.12 = (f32[1032,128]{1,0:T(8,128)}, f32[1032,128]{1,0:T(8,128)}, u32[]{:S(2)}, u32[]{:S(2)}) collective-permute-start(f32[1032,128]{1,0:T(8,128)} %collective-permute-done.4.refs_11_.refs_2_), channel_id=1, source_target_pairs={{0,8},{1,17},{8,0},{9,25},{16,24},{17,1},{24,16},{25,9},{2,10},{3,... | collective-permute-start | bytes 1585160 | tf_op jit(solution)/shard_map/ppermute | solution.py:407
  38.1 14.8 %collective-permute-start.14 = (f32[1032,128]{1,0:T(8,128)}, f32[1032,128]{1,0:T(8,128)S(1)}, u32[]{:S(2)}, u32[]{:S(2)}) collective-permute-start(f32[1032,128]{1,0:T(8,128)} %collective-permute-done.4.refs_11_.refs_2_), channel_id=1, source_target_pairs={{0,1},{1,0},{2,3},{3,2},{4,5},{5,4},{6,7},{7,6},{8,9},{9,8},{10,11... | collective-permute-start | bytes 1585160 | tf_op jit(solution)/shard_map/ppermute | solution.py:415
  39.5 13.5 %collective-permute-start.15 = (f32[1032,128]{1,0:T(8,128)S(1)}, f32[1032,128]{1,0:T(8,128)S(1)}, u32[]{:S(2)}, u32[]{:S(2)}) collective-permute-start(f32[1032,128]{1,0:T(8,128)S(1)} %collective-permute-done.5.refs_4_.refs_13_), channel_id=1, source_target_pairs={{0,1},{1,0},{2,3},{3,2},{4,5},{5,4},{6,7},{7,6},{8,9},{9,8},{10,11... | collective-permute-start | bytes 1585160 | tf_op jit(solution)/shard_map/ppermute | solution.py:415
  54.3 20.6 %collective-permute-start.10 = (f32[1032,128]{1,0:T(8,128)}, f32[1032,128]{1,0:T(8,128)}, u32[]{:S(2)}, u32[]{:S(2)}) collective-permute-start(f32[1032,128]{1,0:T(8,128)} %collective-permute-done.6.refs_3_), channel_id=1, source_target_pairs={{0,16},{1,9},{8,24},{9,1},{16,0},{17,25},{24,8},{25,17},{2,18},{3,... | collective-permute-start | bytes 1585160 | tf_op jit(solution)/shard_map/ppermute | solution.py:407
  55.5 19.4 %collective-permute-start.18 = (f32[1032,128]{1,0:T(8,128)}, f32[1032,128]{1,0:T(8,128)}, u32[]{:S(2)}, u32[]{:S(2)}) collective-permute-start(f32[1032,128]{1,0:T(8,128)} %collective-permute-done.4.refs_11_.refs_2_), channel_id=1, source_target_pairs={{0,16},{1,9},{8,24},{9,1},{16,0},{17,25},{24,8},{25,17},{2,18},{3,... | collective-permute-start | bytes 1585160 | tf_op jit(solution)/shard_map/ppermute | solution.py:407
  55.8 19.1 %collective-permute-start.17 = (f32[1032,128]{1,0:T(8,128)}, f32[1032,128]{1,0:T(8,128)}, u32[]{:S(2)}, u32[]{:S(2)}) collective-permute-start(f32[1032,128]{1,0:T(8,128)} %collective-permute-done.11.refs_12_.refs_2_), channel_id=1, source_target_pairs={{0,8},{1,17},{8,0},{9,25},{16,24},{17,1},{24,16},{25,9},{2,10},{3,... | collective-permute-start | bytes 1585160 | tf_op jit(solution)/shard_map/ppermute | solution.py:407
  55.8 19.1 %collective-permute-start.20 = (f32[1032,128]{1,0:T(8,128)}, f32[1032,128]{1,0:T(8,128)}, u32[]{:S(2)}, u32[]{:S(2)}) collective-permute-start(f32[1032,128]{1,0:T(8,128)} %collective-permute-done.12.refs_3_), channel_id=1, source_target_pairs={{0,1},{1,0},{2,3},{3,2},{4,5},{5,4},{6,7},{7,6},{8,9},{9,8},{10,11... | collective-permute-start | bytes 1585160 | tf_op jit(solution)/shard_map/ppermute | solution.py:415
  58.5 16.4 %collective-permute-start.21 = (f32[1032,128]{1,0:T(8,128)}, f32[1032,128]{1,0:T(8,128)}, u32[]{:S(2)}, u32[]{:S(2)}) collective-permute-start(f32[1032,128]{1,0:T(8,128)} %collective-permute-done.13.refs_4_), channel_id=1, source_target_pairs={{0,1},{1,0},{2,3},{3,2},{4,5},{5,4},{6,7},{7,6},{8,9},{9,8},{10,11... | collective-permute-start | bytes 1585160 | tf_op jit(solution)/shard_map/ppermute | solution.py:415
  76.0 13.9 %collective-permute-start.23 = (f32[1032,128]{1,0:T(8,128)}, f32[1032,128]{1,0:T(8,128)S(1)}, u32[]{:S(2)}, u32[]{:S(2)}) collective-permute-start(f32[1032,128]{1,0:T(8,128)} %collective-permute-done.12.refs_3_), channel_id=1, source_target_pairs={{0,16},{1,9},{8,24},{9,1},{16,0},{17,25},{24,8},{25,17},{2,18},{3,... | collective-permute-start | bytes 1585160 | tf_op jit(solution)/shard_map/ppermute | solution.py:407
  77.2 13.0 %collective-permute-start.24 = (f32[1032,128]{1,0:T(8,128)}, f32[1032,128]{1,0:T(8,128)S(1)}, u32[]{:S(2)}, u32[]{:S(2)}) collective-permute-start(f32[1032,128]{1,0:T(8,128)} %collective-permute-done.11.refs_12_.refs_2_), channel_id=1, source_target_pairs={{0,16},{1,9},{8,24},{9,1},{16,0},{17,25},{24,8},{25,17},{2,18},{3,... | collective-permute-start | bytes 1585160 | tf_op jit(solution)/shard_map/ppermute | solution.py:407
  77.4 12.8 %collective-permute-start.26 = (f32[1032,128]{1,0:T(8,128)}, f32[1032,128]{1,0:T(8,128)S(1)}, u32[]{:S(2)}, u32[]{:S(2)}) collective-permute-start(f32[1032,128]{1,0:T(8,128)} %collective-permute-done.17.refs_3_), channel_id=1, source_target_pairs={{0,1},{1,0},{2,3},{3,2},{4,5},{5,4},{6,7},{7,6},{8,9},{9,8},{10,11... | collective-permute-start | bytes 1585160 | tf_op jit(solution)/shard_map/ppermute | solution.py:415
  91.2 13.4 %collective-permute-start.22 = (f32[1032,128]{1,0:T(8,128)}, f32[1032,128]{1,0:T(8,128)S(1)}, u32[]{:S(2)}, u32[]{:S(2)}) collective-permute-start(f32[1032,128]{1,0:T(8,128)} %collective-permute-done.17.refs_3_), channel_id=1, source_target_pairs={{0,16},{1,9},{8,24},{9,1},{16,0},{17,25},{24,8},{25,17},{2,18},{3,... | collective-permute-start | bytes 1585160 | tf_op jit(solution)/shard_map/ppermute | solution.py:407
  92.4 13.4 %collective-permute-start.29 = (f32[1032,128]{1,0:T(8,128)}, f32[1032,128]{1,0:T(8,128)}, u32[]{:S(2)}, u32[]{:S(2)}) collective-permute-start(f32[1032,128]{1,0:T(8,128)} %collective-permute-done.17.refs_3_), channel_id=1, source_target_pairs={{0,17},{1,8},{8,25},{9,0},{16,1},{17,24},{24,9},{25,16},{2,19},{3,... | collective-permute-start | bytes 1585160 | tf_op jit(solution)/shard_map/ppermute | solution.py:407
  92.5 13.3 %collective-permute-start.30 = (f32[1032,128]{1,0:T(8,128)S(1)}, f32[1032,128]{1,0:T(8,128)}, u32[]{:S(2)}, u32[]{:S(2)}) collective-permute-start(f32[1032,128]{1,0:T(8,128)S(1)} %collective-permute-done.24.refs_4_), channel_id=1, source_target_pairs={{0,1},{1,0},{2,3},{3,2},{4,5},{5,4},{6,7},{7,6},{8,9},{9,8},{10,11... | collective-permute-start | bytes 1585160 | tf_op jit(solution)/shard_map/ppermute | solution.py:415
  (25 other events, 355.9 us)

commit v5 on v4

--- a/solution.py
+++ b/solution.py
@@ -8,7 +8,7 @@
 from jax.sharding import PartitionSpec as P
 
 ROW_BLOCKS = 12
-GROUP = 4
+GROUP = 8
 CUBES = 8
 CHUNK = 128
 STRIP = 384

time: 118 us -> 117 us (level)
  transfers between devices with their start and end apart: 31 -> 31, of which waited for: 9 -> 8; matrix products, arithmetic and copies ran while one was open for 1% -> 1% of each run, Pallas kernels for 33% -> 33%
where the time goes in v5:
time: 117 us
  Pallas kernels  50.3 us (43%)
  waiting for transfers between devices  33.1 us (28%)
  starting transfers between devices  29 us (25%)
  other arithmetic  2.36 us (2%)
  local copies, waits for them, and re-layouts  1.37 us (1%)
    pallas_call x3, Pallas kernels, tile_call(): return (call(table, left, *arrays, *extra), lefts)  34.3 us
    ppermute x3, waiting for transfers between devices, ring(): return lax.ppermute(y, 'col', [(i, (i + 1) % n_col) for i in range(n_col)])  22.4 us
    ppermute x15, starting transfers between devices, sibling(): lax.ppermute(y, 'layer', [(i, n_layer - 1 - i) for i in range(n_layer)])  16.4 us
    pallas_call x1, Pallas kernels, tile_call(): out, left, table = call(where, *arrays, *built)  16 us
    ppermute x13, waiting for transfers between devices, flip(): return lambda y: lax.ppermute(y, ('row', 'layer'), pairs)  9.96 us
    ppermute x13, starting transfers between devices, flip(): return lambda y: lax.ppermute(y, ('row', 'layer'), pairs)  9.07 us
    ppermute x3, starting transfers between devices, ring(): return lax.ppermute(y, 'col', [(i, (i + 1) % n_col) for i in range(n_col)])  3.53 us
  transfers between devices with their start and end apart: 31, of which 8 were waited for; matrix products, arithmetic and copies ran while one was open for 1% of the time, Pallas kernels for 33%

profile of v5, /device:TPU:1, one launch (start us, length us, event | category | flops | bytes accessed | tf_op | source)
XLA Modules:
  0.0 117.0 jit_solution(8036790421951701992)
XLA Ops:
  2.4 2.2 %collective-permute-start = (f32[1032,128]{1,0:T(8,128)S(1)}, f32[1032,128]{1,0:T(8,128)S(1)}, u32[]{:S(2)}, u32[]{:S(2)}) collective-permute-start(f32[1032,128]{1,0:T(8,128)S(1)} %select_maximum_fusion.refs_1_.refs_9_.refs_10_), channel_id=1, source_target_pairs={{0,2},{2,4},{4,6},{6,0},{1,3},{3,5},{5,7},{7,1},{8,10},{10,12},{12... | collective-permute-start | bytes 1585160 | tf_op jit(solution)/shard_map/ppermute | solution.py:412
  4.6 1.2 %collective-permute-start.1 = (f32[1032,128]{1,0:T(8,128)S(1)}, f32[1032,128]{1,0:T(8,128)S(1)}, u32[]{:S(2)}, u32[]{:S(2)}) collective-permute-start(f32[1032,128]{1,0:T(8,128)S(1)} %select_maximum_fusion.refs_1_.refs_9_.refs_10_), channel_id=1, source_target_pairs={{0,8},{1,17},{8,0},{9,25},{16,24},{17,1},{24,16},{25,9},{2,10},{3,... | collective-permute-start | bytes 1585160 | tf_op jit(solution)/shard_map/ppermute | solution.py:407
  5.8 1.2 %collective-permute-start.2 = (f32[1032,128]{1,0:T(8,128)S(1)}, f32[1032,128]{1,0:T(8,128)S(1)}, u32[]{:S(2)}, u32[]{:S(2)}) collective-permute-start(f32[1032,128]{1,0:T(8,128)S(1)} %select_maximum_fusion.refs_1_.refs_9_.refs_10_), channel_id=1, source_target_pairs={{0,16},{1,9},{8,24},{9,1},{16,0},{17,25},{24,8},{25,17},{2,18},{3,... | collective-permute-start | bytes 1585160 | tf_op jit(solution)/shard_map/ppermute | solution.py:407
  7.0 1.5 %collective-permute-start.3 = (f32[1032,128]{1,0:T(8,128)S(1)}, f32[1032,128]{1,0:T(8,128)S(1)}, u32[]{:S(2)}, u32[]{:S(2)}) collective-permute-start(f32[1032,128]{1,0:T(8,128)S(1)} %select_maximum_fusion.refs_1_.refs_9_.refs_10_), channel_id=1, source_target_pairs={{0,1},{1,0},{2,3},{3,2},{4,5},{5,4},{6,7},{7,6},{8,9},{9,8},{10,11... | collective-permute-start | bytes 1585160 | tf_op jit(solution)/shard_map/ppermute | solution.py:415
  8.6 9.8 %collective-permute-done.refs_10_.refs_2_ = f32[1032,128]{1,0:T(8,128)S(1)} collective-permute-done((f32[1032,128]{1,0:T(8,128)S(1)}, f32[1032,128]{1,0:T(8,128)S(1)}, u32[]{:S(2)}, u32[]{:S(2)}) %collective-permute-start) | collective-permute-done | bytes 528416 | tf_op jit(solution)/shard_map/ppermute | solution.py:412
  18.4 1.3 %collective-permute-done.2.refs_3_.refs_12_ = f32[1032,128]{1,0:T(8,128)S(1)} collective-permute-done((f32[1032,128]{1,0:T(8,128)S(1)}, f32[1032,128]{1,0:T(8,128)S(1)}, u32[]{:S(2)}, u32[]{:S(2)}) %collective-permute-start.2) | collective-permute-done | bytes 528416 | tf_op jit(solution)/shard_map/ppermute | solution.py:407
  19.7 1.3 %collective-permute-start.4 = (f32[1032,128]{1,0:T(8,128)S(1)}, f32[1032,128]{1,0:T(8,128)}, u32[]{:S(2)}, u32[]{:S(2)}) collective-permute-start(f32[1032,128]{1,0:T(8,128)S(1)} %collective-permute-done.refs_10_.refs_2_), channel_id=1, source_target_pairs={{0,2},{2,4},{4,6},{6,0},{1,3},{3,5},{5,7},{7,1},{8,10},{10,12},{12... | collective-permute-start | bytes 1585160 | tf_op jit(solution)/shard_map/ppermute | solution.py:412
  21.0 1.2 %collective-permute-start.5 = (f32[1032,128]{1,0:T(8,128)S(1)}, f32[1032,128]{1,0:T(8,128)S(1)}, u32[]{:S(2)}, u32[]{:S(2)}) collective-permute-start(f32[1032,128]{1,0:T(8,128)S(1)} %collective-permute-done.1.refs_2_.refs_11_), channel_id=1, source_target_pairs={{0,16},{1,9},{8,24},{9,1},{16,0},{17,25},{24,8},{25,17},{2,18},{3,... | collective-permute-start | bytes 1585160 | tf_op jit(solution)/shard_map/ppermute | solution.py:407
  22.3 1.7 %collective-permute-start.7 = (f32[1032,128]{1,0:T(8,128)S(1)}, f32[1032,128]{1,0:T(8,128)S(1)}, u32[]{:S(2)}, u32[]{:S(2)}) collective-permute-start(f32[1032,128]{1,0:T(8,128)S(1)} %collective-permute-done.refs_10_.refs_2_), channel_id=1, source_target_pairs={{0,1},{1,0},{2,3},{3,2},{4,5},{5,4},{6,7},{7,6},{8,9},{9,8},{10,11... | collective-permute-start | bytes 1585160 | tf_op jit(solution)/shard_map/ppermute | solution.py:415
  23.9 10.7 %collective-permute-done.4.refs_11_.refs_2_ = f32[1032,128]{1,0:T(8,128)} collective-permute-done((f32[1032,128]{1,0:T(8,128)S(1)}, f32[1032,128]{1,0:T(8,128)}, u32[]{:S(2)}, u32[]{:S(2)}) %collective-permute-start.4) | collective-permute-done | bytes 528416 | tf_op jit(solution)/shard_map/ppermute | solution.py:412
  34.6 1.5 %collective-permute-start.9 = (f32[1032,128]{1,0:T(8,128)S(1)}, f32[1032,128]{1,0:T(8,128)S(1)}, u32[]{:S(2)}, u32[]{:S(2)}) collective-permute-start(f32[1032,128]{1,0:T(8,128)S(1)} %collective-permute-done.2.refs_3_.refs_12_), channel_id=1, source_target_pairs={{0,1},{1,0},{2,3},{3,2},{4,5},{5,4},{6,7},{7,6},{8,9},{9,8},{10,11... | collective-permute-start | bytes 1585160 | tf_op jit(solution)/shard_map/ppermute | solution.py:415
  36.1 1.2 %collective-permute-start.13 = (f32[1032,128]{1,0:T(8,128)S(1)}, f32[1032,128]{1,0:T(8,128)}, u32[]{:S(2)}, u32[]{:S(2)}) collective-permute-start(f32[1032,128]{1,0:T(8,128)S(1)} %collective-permute-done.refs_10_.refs_2_), channel_id=1, source_target_pairs={{0,16},{1,9},{8,24},{9,1},{16,0},{17,25},{24,8},{25,17},{2,18},{3,... | collective-permute-start | bytes 1585160 | tf_op jit(solution)/shard_map/ppermute | solution.py:407
  38.1 1.4 %collective-permute-start.14 = (f32[1032,128]{1,0:T(8,128)}, f32[1032,128]{1,0:T(8,128)S(1)}, u32[]{:S(2)}, u32[]{:S(2)}) collective-permute-start(f32[1032,128]{1,0:T(8,128)} %collective-permute-done.4.refs_11_.refs_2_), channel_id=1, source_target_pairs={{0,1},{1,0},{2,3},{3,2},{4,5},{5,4},{6,7},{7,6},{8,9},{9,8},{10,11... | collective-permute-start | bytes 1585160 | tf_op jit(solution)/shard_map/ppermute | solution.py:415
  39.5 7.4 %collective-permute-done.13.refs_4_ = f32[1032,128]{1,0:T(8,128)} collective-permute-done((f32[1032,128]{1,0:T(8,128)S(1)}, f32[1032,128]{1,0:T(8,128)}, u32[]{:S(2)}, u32[]{:S(2)}) %collective-permute-start.13) | collective-permute-done | bytes 528416 | tf_op jit(solution)/shard_map/ppermute | solution.py:407
  46.9 4.1 %collective-permute-start.16 = (f32[1032,128]{1,0:T(8,128)}, f32[1032,128]{1,0:T(8,128)S(1)}, u32[]{:S(2)}, u32[]{:S(2)}) collective-permute-start(f32[1032,128]{1,0:T(8,128)} %collective-permute-done.6.refs_3_), channel_id=1, source_target_pairs={{0,1},{1,0},{2,3},{3,2},{4,5},{5,4},{6,7},{7,6},{8,9},{9,8},{10,11... | collective-permute-start | bytes 1585160 | tf_op jit(solution)/shard_map/ppermute | solution.py:415
  51.0 1.9 %collective-permute-done.11.refs_12_.refs_2_ = f32[1032,128]{1,0:T(8,128)} collective-permute-done((f32[1032,128]{1,0:T(8,128)}, f32[1032,128]{1,0:T(8,128)}, u32[]{:S(2)}, u32[]{:S(2)}) %collective-permute-start.11) | collective-permute-done | bytes 528416 | tf_op jit(solution)/shard_map/ppermute | solution.py:412
  53.0 1.3 %collective-permute-start.19 = (f32[1032,128]{1,0:T(8,128)}, f32[1032,128]{1,0:T(8,128)}, u32[]{:S(2)}, u32[]{:S(2)}) collective-permute-start(f32[1032,128]{1,0:T(8,128)} %collective-permute-done.11.refs_12_.refs_2_), channel_id=1, source_target_pairs={{0,1},{1,0},{2,3},{3,2},{4,5},{5,4},{6,7},{7,6},{8,9},{9,8},{10,11... | collective-permute-start | bytes 1585160 | tf_op jit(solution)/shard_map/ppermute | solution.py:415
  55.8 2.8 %collective-permute-start.20 = (f32[1032,128]{1,0:T(8,128)}, f32[1032,128]{1,0:T(8,128)}, u32[]{:S(2)}, u32[]{:S(2)}) collective-permute-start(f32[1032,128]{1,0:T(8,128)} %collective-permute-done.12.refs_3_), channel_id=1, source_target_pairs={{0,1},{1,0},{2,3},{3,2},{4,5},{5,4},{6,7},{7,6},{8,9},{9,8},{10,11... | collective-permute-start | bytes 1585160 | tf_op jit(solution)/shard_map/ppermute | solution.py:415
  59.3 16.0 %tiles_0.1 = (f32[768,1536]{1,0:T(8,128)}, bf16[64,128,256]{2,1,0:T(8,128)(2,1)}, s32[180]{0:T(256)}) custom-call(s32[3]{0:T(128)} %pad_add_fusion.refs_0_, f32[1032,128]{1,0:T(8,128)} %copy-done, f32[1032,128]{1,0:T(8,128)} %copy-done.2, f32[1032,128]{1,0:T(8,128)} %copy-done.3, f32[1032,128]{1,0:T(8,128)} %copy-done.4, f32[1032,128]{1,0:T(8,128)} %copy-done.1, ...), custom_call_target="tpu_custom_call" | custom-call | tf_op jit(solution)/shard_map/tiles_0/pallas_call | solution.py:389
  76.0 1.2 %collective-permute-start.23 = (f32[1032,128]{1,0:T(8,128)}, f32[1032,128]{1,0:T(8,128)S(1)}, u32[]{:S(2)}, u32[]{:S(2)}) collective-permute-start(f32[1032,128]{1,0:T(8,128)} %collective-permute-done.12.refs_3_), channel_id=1, source_target_pairs={{0,16},{1,9},{8,24},{9,1},{16,0},{17,25},{24,8},{25,17},{2,18},{3,... | collective-permute-start | bytes 1585160 | tf_op jit(solution)/shard_map/ppermute | solution.py:407
  78.9 11.4 %tiles_1.1.refs_18_ = f32[768,1536]{1,0:T(8,128)} custom-call(s32[180]{0:T(256)} %get-tuple-element.79.refs_0_, bf16[64,128,256]{2,1,0:T(8,128)(2,1)} %get-tuple-element.80.refs_1_, f32[1032,128]{1,0:T(8,128)} %copy-done.8, f32[1032,128]{1,0:T(8,128)} %collective-permute-done.6.refs_3_, f32[1032,128]{1,0:T(8,128)} %collective-permute-done.13.refs_4_, ...), custom_call_target="tpu_custom_call" | custom-call | tf_op jit(solution)/shard_map/tiles_1/pallas_call | solution.py:392
  91.2 1.2 %collective-permute-start.22 = (f32[1032,128]{1,0:T(8,128)}, f32[1032,128]{1,0:T(8,128)S(1)}, u32[]{:S(2)}, u32[]{:S(2)}) collective-permute-start(f32[1032,128]{1,0:T(8,128)} %collective-permute-done.17.refs_3_), channel_id=1, source_target_pairs={{0,16},{1,9},{8,24},{9,1},{16,0},{17,25},{24,8},{25,17},{2,18},{3,... | collective-permute-start | bytes 1585160 | tf_op jit(solution)/shard_map/ppermute | solution.py:407
  92.9 11.7 %tiles_2.1.refs_18_ = f32[768,1536]{1,0:T(8,128)} custom-call(s32[180]{0:T(256)} %get-tuple-element.79.refs_0_, bf16[64,128,256]{2,1,0:T(8,128)(2,1)} %get-tuple-element.80.refs_1_, f32[1032,128]{1,0:T(8,128)} %collective-permute-done.4.refs_11_.refs_2_, f32[1032,128]{1,0:T(8,128)} %collective-permute-done.12.refs_3_, ...), custom_call_target="tpu_custom_call" | custom-call | tf_op jit(solution)/shard_map/tiles_2/pallas_call | solution.py:392
  105.8 11.2 %tiles_3.1 = f32[768,1536]{1,0:T(8,128)} custom-call(s32[180]{0:T(256)} %get-tuple-element.79.refs_0_, bf16[64,128,256]{2,1,0:T(8,128)(2,1)} %get-tuple-element.80.refs_1_, f32[1032,128]{1,0:T(8,128)} %collective-permute-done.11.refs_12_.refs_2_, f32[1032,128]{1,0:T(8,128)} %collective-permute-done.17.refs_3_, f32[1032,128]{1,0:T(8,128)} %copy-done.12, ...), custom_call_target="tpu_custom_call" | custom-call | tf_op jit(solution)/shard_map/tiles_3/pallas_call | solution.py:392
  (81 shorter events, 9.6 us)
Async XLA Ops:
  2.4 15.9 %collective-permute-start = (f32[1032,128]{1,0:T(8,128)S(1)}, f32[1032,128]{1,0:T(8,128)S(1)}, u32[]{:S(2)}, u32[]{:S(2)}) collective-permute-start(f32[1032,128]{1,0:T(8,128)S(1)} %select_maximum_fusion.refs_1_.refs_9_.refs_10_), channel_id=1, source_target_pairs={{0,2},{2,4},{4,6},{6,0},{1,3},{3,5},{5,7},{7,1},{8,10},{10,12},{12... | collective-permute-start | bytes 1585160 | tf_op jit(solution)/shard_map/ppermute | solution.py:412
  4.6 13.8 %collective-permute-start.1 = (f32[1032,128]{1,0:T(8,128)S(1)}, f32[1032,128]{1,0:T(8,128)S(1)}, u32[]{:S(2)}, u32[]{:S(2)}) collective-permute-start(f32[1032,128]{1,0:T(8,128)S(1)} %select_maximum_fusion.refs_1_.refs_9_.refs_10_), channel_id=1, source_target_pairs={{0,8},{1,17},{8,0},{9,25},{16,24},{17,1},{24,16},{25,9},{2,10},{3,... | collective-permute-start | bytes 1585160 | tf_op jit(solution)/shard_map/ppermute | solution.py:407
  5.8 13.9 %collective-permute-start.2 = (f32[1032,128]{1,0:T(8,128)S(1)}, f32[1032,128]{1,0:T(8,128)S(1)}, u32[]{:S(2)}, u32[]{:S(2)}) collective-permute-start(f32[1032,128]{1,0:T(8,128)S(1)} %select_maximum_fusion.refs_1_.refs_9_.refs_10_), channel_id=1, source_target_pairs={{0,16},{1,9},{8,24},{9,1},{16,0},{17,25},{24,8},{25,17},{2,18},{3,... | collective-permute-start | bytes 1585160 | tf_op jit(solution)/shard_map/ppermute | solution.py:407
  7.0 12.7 %collective-permute-start.3 = (f32[1032,128]{1,0:T(8,128)S(1)}, f32[1032,128]{1,0:T(8,128)S(1)}, u32[]{:S(2)}, u32[]{:S(2)}) collective-permute-start(f32[1032,128]{1,0:T(8,128)S(1)} %select_maximum_fusion.refs_1_.refs_9_.refs_10_), channel_id=1, source_target_pairs={{0,1},{1,0},{2,3},{3,2},{4,5},{5,4},{6,7},{7,6},{8,9},{9,8},{10,11... | collective-permute-start | bytes 1585160 | tf_op jit(solution)/shard_map/ppermute | solution.py:415
  19.7 14.9 %collective-permute-start.4 = (f32[1032,128]{1,0:T(8,128)S(1)}, f32[1032,128]{1,0:T(8,128)}, u32[]{:S(2)}, u32[]{:S(2)}) collective-permute-start(f32[1032,128]{1,0:T(8,128)S(1)} %collective-permute-done.refs_10_.refs_2_), channel_id=1, source_target_pairs={{0,2},{2,4},{4,6},{6,0},{1,3},{3,5},{5,7},{7,1},{8,10},{10,12},{12... | collective-permute-start | bytes 1585160 | tf_op jit(solution)/shard_map/ppermute | solution.py:412
  21.0 15.0 %collective-permute-start.5 = (f32[1032,128]{1,0:T(8,128)S(1)}, f32[1032,128]{1,0:T(8,128)S(1)}, u32[]{:S(2)}, u32[]{:S(2)}) collective-permute-start(f32[1032,128]{1,0:T(8,128)S(1)} %collective-permute-done.1.refs_2_.refs_11_), channel_id=1, source_target_pairs={{0,16},{1,9},{8,24},{9,1},{16,0},{17,25},{24,8},{25,17},{2,18},{3,... | collective-permute-start | bytes 1585160 | tf_op jit(solution)/shard_map/ppermute | solution.py:407
  22.3 15.0 %collective-permute-start.6 = (f32[1032,128]{1,0:T(8,128)S(1)}, f32[1032,128]{1,0:T(8,128)}, u32[]{:S(2)}, u32[]{:S(2)}) collective-permute-start(f32[1032,128]{1,0:T(8,128)S(1)} %collective-permute-done.refs_10_.refs_2_), channel_id=1, source_target_pairs={{0,8},{1,17},{8,0},{9,25},{16,24},{17,1},{24,16},{25,9},{2,10},{3,... | collective-permute-start | bytes 1585160 | tf_op jit(solution)/shard_map/ppermute | solution.py:407
  22.3 15.0 %collective-permute-start.7 = (f32[1032,128]{1,0:T(8,128)S(1)}, f32[1032,128]{1,0:T(8,128)S(1)}, u32[]{:S(2)}, u32[]{:S(2)}) collective-permute-start(f32[1032,128]{1,0:T(8,128)S(1)} %collective-permute-done.refs_10_.refs_2_), channel_id=1, source_target_pairs={{0,1},{1,0},{2,3},{3,2},{4,5},{5,4},{6,7},{7,6},{8,9},{9,8},{10,11... | collective-permute-start | bytes 1585160 | tf_op jit(solution)/shard_map/ppermute | solution.py:415
  23.9 13.4 %collective-permute-start.8 = (f32[1032,128]{1,0:T(8,128)S(1)}, f32[1032,128]{1,0:T(8,128)S(1)}, u32[]{:S(2)}, u32[]{:S(2)}) collective-permute-start(f32[1032,128]{1,0:T(8,128)S(1)} %collective-permute-done.1.refs_2_.refs_11_), channel_id=1, source_target_pairs={{0,1},{1,0},{2,3},{3,2},{4,5},{5,4},{6,7},{7,6},{8,9},{9,8},{10,11... | collective-permute-start | bytes 1585160 | tf_op jit(solution)/shard_map/ppermute | solution.py:415
  37.6 15.3 %collective-permute-start.11 = (f32[1032,128]{1,0:T(8,128)}, f32[1032,128]{1,0:T(8,128)}, u32[]{:S(2)}, u32[]{:S(2)}) collective-permute-start(f32[1032,128]{1,0:T(8,128)} %collective-permute-done.4.refs_11_.refs_2_), channel_id=1, source_target_pairs={{0,2},{2,4},{4,6},{6,0},{1,3},{3,5},{5,7},{7,1},{8,10},{10,12},{12... | collective-permute-start | bytes 1585160 | tf_op jit(solution)/shard_map/ppermute | solution.py:412
  37.6 15.3 %collective-permute-start.12 = (f32[1032,128]{1,0:T(8,128)}, f32[1032,128]{1,0:T(8,128)}, u32[]{:S(2)}, u32[]{:S(2)}) collective-permute-start(f32[1032,128]{1,0:T(8,128)} %collective-permute-done.4.refs_11_.refs_2_), channel_id=1, source_target_pairs={{0,8},{1,17},{8,0},{9,25},{16,24},{17,1},{24,16},{25,9},{2,10},{3,... | collective-permute-start | bytes 1585160 | tf_op jit(solution)/shard_map/ppermute | solution.py:407
  38.1 14.8 %collective-permute-start.14 = (f32[1032,128]{1,0:T(8,128)}, f32[1032,128]{1,0:T(8,128)S(1)}, u32[]{:S(2)}, u32[]{:S(2)}) collective-permute-start(f32[1032,128]{1,0:T(8,128)} %collective-permute-done.4.refs_11_.refs_2_), channel_id=1, source_target_pairs={{0,1},{1,0},{2,3},{3,2},{4,5},{5,4},{6,7},{7,6},{8,9},{9,8},{10,11... | collective-permute-start | bytes 1585160 | tf_op jit(solution)/shard_map/ppermute | solution.py:415
  39.5 13.5 %collective-permute-start.15 = (f32[1032,128]{1,0:T(8,128)S(1)}, f32[1032,128]{1,0:T(8,128)S(1)}, u32[]{:S(2)}, u32[]{:S(2)}) collective-permute-start(f32[1032,128]{1,0:T(8,128)S(1)} %collective-permute-done.5.refs_4_.refs_13_), channel_id=1, source_target_pairs={{0,1},{1,0},{2,3},{3,2},{4,5},{5,4},{6,7},{7,6},{8,9},{9,8},{10,11... | collective-permute-start | bytes 1585160 | tf_op jit(solution)/shard_map/ppermute | solution.py:415
  54.3 21.0 %collective-permute-start.10 = (f32[1032,128]{1,0:T(8,128)}, f32[1032,128]{1,0:T(8,128)}, u32[]{:S(2)}, u32[]{:S(2)}) collective-permute-start(f32[1032,128]{1,0:T(8,128)} %collective-permute-done.6.refs_3_), channel_id=1, source_target_pairs={{0,16},{1,9},{8,24},{9,1},{16,0},{17,25},{24,8},{25,17},{2,18},{3,... | collective-permute-start | bytes 1585160 | tf_op jit(solution)/shard_map/ppermute | solution.py:407
  55.5 19.8 %collective-permute-start.18 = (f32[1032,128]{1,0:T(8,128)}, f32[1032,128]{1,0:T(8,128)}, u32[]{:S(2)}, u32[]{:S(2)}) collective-permute-start(f32[1032,128]{1,0:T(8,128)} %collective-permute-done.4.refs_11_.refs_2_), channel_id=1, source_target_pairs={{0,16},{1,9},{8,24},{9,1},{16,0},{17,25},{24,8},{25,17},{2,18},{3,... | collective-permute-start | bytes 1585160 | tf_op jit(solution)/shard_map/ppermute | solution.py:407
  55.8 19.5 %collective-permute-start.17 = (f32[1032,128]{1,0:T(8,128)}, f32[1032,128]{1,0:T(8,128)}, u32[]{:S(2)}, u32[]{:S(2)}) collective-permute-start(f32[1032,128]{1,0:T(8,128)} %collective-permute-done.11.refs_12_.refs_2_), channel_id=1, source_target_pairs={{0,8},{1,17},{8,0},{9,25},{16,24},{17,1},{24,16},{25,9},{2,10},{3,... | collective-permute-start | bytes 1585160 | tf_op jit(solution)/shard_map/ppermute | solution.py:407
  55.8 19.5 %collective-permute-start.20 = (f32[1032,128]{1,0:T(8,128)}, f32[1032,128]{1,0:T(8,128)}, u32[]{:S(2)}, u32[]{:S(2)}) collective-permute-start(f32[1032,128]{1,0:T(8,128)} %collective-permute-done.12.refs_3_), channel_id=1, source_target_pairs={{0,1},{1,0},{2,3},{3,2},{4,5},{5,4},{6,7},{7,6},{8,9},{9,8},{10,11... | collective-permute-start | bytes 1585160 | tf_op jit(solution)/shard_map/ppermute | solution.py:415
  58.5 16.8 %collective-permute-start.21 = (f32[1032,128]{1,0:T(8,128)}, f32[1032,128]{1,0:T(8,128)}, u32[]{:S(2)}, u32[]{:S(2)}) collective-permute-start(f32[1032,128]{1,0:T(8,128)} %collective-permute-done.13.refs_4_), channel_id=1, source_target_pairs={{0,1},{1,0},{2,3},{3,2},{4,5},{5,4},{6,7},{7,6},{8,9},{9,8},{10,11... | collective-permute-start | bytes 1585160 | tf_op jit(solution)/shard_map/ppermute | solution.py:415
  76.0 14.4 %collective-permute-start.23 = (f32[1032,128]{1,0:T(8,128)}, f32[1032,128]{1,0:T(8,128)S(1)}, u32[]{:S(2)}, u32[]{:S(2)}) collective-permute-start(f32[1032,128]{1,0:T(8,128)} %collective-permute-done.12.refs_3_), channel_id=1, source_target_pairs={{0,16},{1,9},{8,24},{9,1},{16,0},{17,25},{24,8},{25,17},{2,18},{3,... | collective-permute-start | bytes 1585160 | tf_op jit(solution)/shard_map/ppermute | solution.py:407
  77.2 13.2 %collective-permute-start.24 = (f32[1032,128]{1,0:T(8,128)}, f32[1032,128]{1,0:T(8,128)S(1)}, u32[]{:S(2)}, u32[]{:S(2)}) collective-permute-start(f32[1032,128]{1,0:T(8,128)} %collective-permute-done.11.refs_12_.refs_2_), channel_id=1, source_target_pairs={{0,16},{1,9},{8,24},{9,1},{16,0},{17,25},{24,8},{25,17},{2,18},{3,... | collective-permute-start | bytes 1585160 | tf_op jit(solution)/shard_map/ppermute | solution.py:407
  77.4 12.9 %collective-permute-start.26 = (f32[1032,128]{1,0:T(8,128)}, f32[1032,128]{1,0:T(8,128)S(1)}, u32[]{:S(2)}, u32[]{:S(2)}) collective-permute-start(f32[1032,128]{1,0:T(8,128)} %collective-permute-done.17.refs_3_), channel_id=1, source_target_pairs={{0,1},{1,0},{2,3},{3,2},{4,5},{5,4},{6,7},{7,6},{8,9},{9,8},{10,11... | collective-permute-start | bytes 1585160 | tf_op jit(solution)/shard_map/ppermute | solution.py:415
  91.2 13.4 %collective-permute-start.22 = (f32[1032,128]{1,0:T(8,128)}, f32[1032,128]{1,0:T(8,128)S(1)}, u32[]{:S(2)}, u32[]{:S(2)}) collective-permute-start(f32[1032,128]{1,0:T(8,128)} %collective-permute-done.17.refs_3_), channel_id=1, source_target_pairs={{0,16},{1,9},{8,24},{9,1},{16,0},{17,25},{24,8},{25,17},{2,18},{3,... | collective-permute-start | bytes 1585160 | tf_op jit(solution)/shard_map/ppermute | solution.py:407
  92.4 13.4 %collective-permute-start.29 = (f32[1032,128]{1,0:T(8,128)}, f32[1032,128]{1,0:T(8,128)}, u32[]{:S(2)}, u32[]{:S(2)}) collective-permute-start(f32[1032,128]{1,0:T(8,128)} %collective-permute-done.17.refs_3_), channel_id=1, source_target_pairs={{0,17},{1,8},{8,25},{9,0},{16,1},{17,24},{24,9},{25,16},{2,19},{3,... | collective-permute-start | bytes 1585160 | tf_op jit(solution)/shard_map/ppermute | solution.py:407
  92.5 13.3 %collective-permute-start.30 = (f32[1032,128]{1,0:T(8,128)S(1)}, f32[1032,128]{1,0:T(8,128)}, u32[]{:S(2)}, u32[]{:S(2)}) collective-permute-start(f32[1032,128]{1,0:T(8,128)S(1)} %collective-permute-done.24.refs_4_), channel_id=1, source_target_pairs={{0,1},{1,0},{2,3},{3,2},{4,5},{5,4},{6,7},{7,6},{8,9},{9,8},{10,11... | collective-permute-start | bytes 1585160 | tf_op jit(solution)/shard_map/ppermute | solution.py:415
  (25 other events, 354.5 us)
